TPU v7x, 1024 devices: a whole 4x4x32 slice. The times are simulated.
1024 devices in a mesh: sect: 4 (over x), grp: 64 (over z, core), span: 4 (over y).
Axes of the slice: x: 4, y: 4, z: 32, core: 2. Of those that a mesh axis runs over, the one named last changes fastest.
Arguments:
- grad_out: bfloat16 [5120, 8192], P('grp', 'span'), may hold values from -6 to 6
- destination: int32 [5120], P('grp'), may hold values from 0 to 5119, as said below
- w_down: bfloat16 [5120, 8192], P('sect', 'span'), may hold values from -0.078125 to 0.078125
- pre_act: bfloat16 [5120, 5120], P('grp', ('sect', 'span')), may hold values from -6 to 6
- w_up: bfloat16 [5120, 5120], P(None, ('sect', 'span')), may hold values from -0.078125 to 0.078125
- queries: bfloat16 [20480, 1280], P('grp', ('sect', 'span')), may hold values from -16 to 16
- key_states: bfloat16 [20480, 1280], P('grp', ('sect', 'span')), may hold values from -16 to 16
- value_states: bfloat16 [20480, 1280], P('grp', ('sect', 'span')), may hold values from -6 to 6
- lengths: int32 [192], replicated, may hold values from 1 to 80, 5120 in all
Outputs:
- grad_queries: bfloat16 [20480, 1280], P('grp', ('sect', 'span'))
- grad_keys: bfloat16 [20480, 1280], P('grp', ('sect', 'span'))
- grad_values: bfloat16 [20480, 1280], P('grp', ('sect', 'span'))
Inputs may be any that keep to these rules, and one draw needn't show every extreme that they name: `destination`: a permutation of the merged tokens; the merged tokens on one index of grp go to exactly 40 indices of grp, exactly 2 to each. `lengths`: an image has 4 patches for each merged token; images lie one after another along the merged tokens.
All inputs are finite; a program needn't handle non-finite values.
Results may differ from a plain program's by a relative error of at most 0.015.
Values may be sent and summed in bfloat16 or wider, within the bound.
A program may use at most 64 MiB of HBM per device.

v0:
```python
import jax
import jax.numpy as jnp
from jax import lax
from jax.sharding import PartitionSpec as P

HEAD_DIM = 80


def passed_along(block, axis, distance):
    devices = range(lax.axis_size(axis))
    route = [(i - distance, i) for i in devices if i - distance in devices]
    return lax.ppermute(block, axis, route)


def extended(x, sides, width):
    for axis, dim in sides:
        peers, length = (lax.axis_size(axis), x.shape[dim])
        up = [(i, (i + 1) % peers) for i in range(peers - 1)]
        down = [(j, i) for i, j in up]
        last = lax.slice_in_dim(x, length - width, length, axis=dim)
        first = lax.slice_in_dim(x, 0, width, axis=dim)
        before = lax.ppermute(last, axis, up)
        after = lax.ppermute(first, axis, down)
        x = jnp.concatenate([before, x, after], axis=dim)
    return x


def gelu_slope(values):
    normal_cdf = 0.5 * (1.0 + jax.scipy.special.erf(values * 0.7071067811865476))
    return normal_cdf + values * jnp.exp(-0.5 * values * values) * 0.3989422804014327


def pack_rows(rows, destination, groups):
    row_count = rows.shape[0]
    row_width = rows.shape[1]
    offsets = min(groups, row_count // 2)
    capacity = row_count // offsets
    targets = destination // row_count
    slot_ids = destination % row_count
    matches = (targets[:, None] == jnp.arange(groups, dtype=jnp.int32)[None, :]).astype(jnp.int32)
    send_order = jnp.sum((jnp.cumsum(matches, 0) - 1) * matches, 1)
    buffer_index = targets * capacity + send_order
    packed = jnp.zeros((groups * capacity, row_width), rows.dtype).at[buffer_index].set(rows)
    labels = jnp.full((groups * capacity,), row_count, jnp.int32).at[buffer_index].set(slot_ids)
    return (packed.reshape(groups, capacity, row_width), labels.reshape(groups, capacity))


def unpack_rows(packed, labels, row_count):
    row_width = packed.shape[2]
    flattened = packed.reshape(-1, row_width)
    placed = (
        jnp.zeros((row_count + 1, row_width), packed.dtype).at[labels.reshape(-1)].set(flattened)
    )
    return placed[:row_count]


def send_back(terms, offset_by):
    return passed_along(terms.astype(jnp.bfloat16), "grp", offset_by).astype(terms.dtype)


def on_device(
    grad_out, destination, w_down, pre_act, w_up, queries, key_states, value_states, lengths
):
    groups = lax.axis_size("grp")
    merged_rows = grad_out.shape[0]
    contract_last = (((1,), (1,)), ((), ()))
    packed, labels = pack_rows(grad_out, destination, groups)
    arrived, arrived_ids = (
        lax.all_to_all(packed, "grp", split_axis=0, concat_axis=0, tiled=True),
        lax.all_to_all(labels, "grp", split_axis=0, concat_axis=0, tiled=True),
    )
    grad_enc = unpack_rows(arrived, arrived_ids, merged_rows)
    partial_hidden = lax.dot_general(
        grad_enc, w_down, contract_last, preferred_element_type=jnp.float32
    )
    grad_hidden = lax.psum_scatter(partial_hidden, "span", scatter_dimension=1, tiled=True)
    grad_pre = (grad_hidden * gelu_slope(pre_act.astype(jnp.float32))).astype(jnp.bfloat16)
    head_devices = lax.axis_size(("sect", "span"))
    merge_rows = w_up.shape[0]
    local_hidden = w_up.shape[1]
    head_cols = queries.shape[1]
    heads_here = head_cols // HEAD_DIM
    reordered = (
        w_up.reshape(4, head_devices, head_cols, local_hidden)
        .transpose(1, 0, 2, 3)
        .reshape(merge_rows, local_hidden)
    )
    share = lax.psum_scatter(
        lax.dot_general(reordered, grad_pre, contract_last, preferred_element_type=jnp.float32),
        ("sect", "span"),
        scatter_dimension=0,
        tiled=True,
    )
    patches = 4 * merged_rows
    grad_attn = (
        share.reshape(4, head_cols, merged_rows)
        .transpose(2, 0, 1)
        .reshape(patches, head_cols)
        .astype(jnp.bfloat16)
    )
    stacked = jnp.stack([key_states, value_states])
    widened = extended(stacked, (("grp", 1),), patches)
    near_keys = widened[0].reshape(3 * patches, heads_here, HEAD_DIM)
    near_values = widened[1].reshape(3 * patches, heads_here, HEAD_DIM)
    group_index = lax.axis_index("grp")
    positions = (group_index - 1) * merged_rows + jnp.arange(3 * merged_rows, dtype=jnp.int32)
    boundaries = jnp.cumsum(lengths)
    token_image = jnp.sum((boundaries[None, :] <= positions[:, None]).astype(jnp.int32), 1)
    inside = (positions >= 0) & (positions < merged_rows * groups)
    token_image = jnp.where(inside, token_image, -1)
    key_image = jnp.repeat(token_image, 4)
    query_image = key_image[patches : 2 * patches]
    same_image = query_image[:, None] == key_image[None, :]
    query_heads = queries.reshape(patches, heads_here, HEAD_DIM)
    grad_heads = grad_attn.reshape(patches, heads_here, HEAD_DIM)
    scale = HEAD_DIM ** (-0.5)
    scores = (
        jnp.einsum("qhe,khe->hqk", query_heads, near_keys, preferred_element_type=jnp.float32)
        * scale
    )
    scores = jnp.where(same_image[None], scores, -jnp.inf)
    top_score = jnp.max(scores, -1, keepdims=True)
    weights = jnp.exp(scores - top_score)
    probs = weights / jnp.sum(weights, -1, keepdims=True)
    probs_low = probs.astype(jnp.bfloat16)
    attended = jnp.einsum(
        "hqk,khe->qhe", probs_low, near_values, preferred_element_type=jnp.float32
    )
    row_delta = jnp.sum(grad_heads.astype(jnp.float32) * attended, -1)
    value_part = jnp.einsum(
        "hqk,qhe->khe", probs_low, grad_heads, preferred_element_type=jnp.float32
    )
    grad_probs = jnp.einsum(
        "qhe,khe->hqk", grad_heads, near_values, preferred_element_type=jnp.float32
    )
    grad_scores = (probs * (grad_probs - row_delta.T[:, :, None])).astype(jnp.bfloat16)
    grad_query = (
        jnp.einsum("hqk,khe->qhe", grad_scores, near_keys, preferred_element_type=jnp.float32)
        * scale
    ).astype(jnp.bfloat16)
    key_part = (
        jnp.einsum("hqk,qhe->khe", grad_scores, query_heads, preferred_element_type=jnp.float32)
        * scale
    )
    parts = jnp.stack([key_part, value_part]).reshape(2, 3 * patches, head_cols)
    own_part = parts[:, patches : 2 * patches]
    from_right = send_back(parts[:, :patches], -1)
    from_left = send_back(parts[:, 2 * patches :], 1)
    totals = own_part + from_right + from_left
    return (
        grad_query.reshape(patches, head_cols),
        totals[0].astype(jnp.bfloat16),
        totals[1].astype(jnp.bfloat16),
    )


def solution(mesh):
    placed = (
        P("grp", "span"),
        P("grp"),
        P("sect", "span"),
        P("grp", ("sect", "span")),
        P(None, ("sect", "span")),
        P("grp", ("sect", "span")),
        P("grp", ("sect", "span")),
        P("grp", ("sect", "span")),
        P(),
    )
    return jax.shard_map(
        on_device,
        mesh=mesh,
        in_specs=placed,
        out_specs=(
            P("grp", ("sect", "span")),
            P("grp", ("sect", "span")),
            P("grp", ("sect", "span")),
        ),
        check_vma=False,
    )
```

profile of v0, /device:TPU:1, one launch (start us, length us, event | category | flops | bytes accessed | tf_op | source)
XLA Modules:
  0.0 301.2 jit_solution(17296802296029633692)
XLA Ops:
  7.2 0.7 and_select_fusion
  8.3 0.8 scatter_custom_fusion
  9.1 0.8 all_to_all.9
  9.8 30.4 %all-to-all-start = ((s32[64,1,2]{2,1,0:T(1,128)}), s32[64,1,2]{2,1,0:T(1,128)S(1)}, u32[]{:S(2)}, u32[]{:S(2)}) async-start(s32[64,1,2]{2,1,0:T(1,128)} %bitcast.6), calls=%async_computation | async-start | bytes 65536 | tf_op jit(solution)/shard_map/all_to_all | solution.py:70
  40.3 1.7 scatter_custom_fusion.1
  41.9 1.1 reshape.182
  43.1 19.5 %all-to-all-done = s32[64,1,2]{2,1,0:T(1,128)S(1)} async-done(((s32[64,1,2]{2,1,0:T(1,128)}), s32[64,1,2]{2,1,0:T(1,128)S(1)}, u32[]{:S(2)}, u32[]{:S(2)}) %all-to-all-start) | async-done | bytes 544 | tf_op jit(solution)/shard_map/all_to_all | solution.py:70
  62.6 5.7 %all-to-all-start.1 = ((bf16[64,2,2048]{2,1,0:T(2,128)(2,1)}), bf16[64,2,2048]{2,1,0:T(2,128)(2,1)S(1)}, u32[]{:S(2)}, u32[]{:S(2)}) async-start(bf16[64,2,2048]{2,1,0:T(2,128)(2,1)} %reshape.182), calls=%async_computation.1 | async-start | bytes 1048576 | tf_op jit(solution)/shard_map/all_to_all | solution.py:69
  68.3 0.5 broadcast.79
  68.8 0.7 reduce.10
  69.7 62.9 %all-to-all-done.1 = bf16[64,2,2048]{2,1,0:T(2,128)(2,1)S(1)} async-done(((bf16[64,2,2048]{2,1,0:T(2,128)(2,1)}), bf16[64,2,2048]{2,1,0:T(2,128)(2,1)S(1)}, u32[]{:S(2)}, u32[]{:S(2)}) %all-to-all-start.1) | async-done | bytes 524320 | tf_op jit(solution)/shard_map/all_to_all | solution.py:69
  132.9 2.0 scatter_custom_fusion.2
  134.9 5.1 %convolution_bitcast_fusion.1 = f32[1280,80]{1,0:T(8,128)} fusion(bf16[1280,2048]{1,0:T(8,128)(2,1)} %param.11, bf16[81,2048]{1,0:T(8,128)(2,1)} %scatter_custom_fusion.2), kind=kOutput, calls=%fused_computation.4 | convolution fusion | flops 419430400 | bytes 5980160
  140.1 3.7 %copy.21 = bf16[5120,320]{1,0:T(8,128)(2,1)} copy(bf16[5120,320]{0,1:T(8,128)(2,1)S(1)} %copy-done.1) | data formatting | bytes 6553600 | tf_op args[4]
  143.8 4.6 %copy.22 = bf16[16,4,80,320]{3,2,1,0:T(8,128)(2,1)} copy(bf16[16,4,80,320]{3,2,0,1:T(8,128)(2,1)} %bitcast.86) | data formatting | bytes 6553600 | tf_op jit(solution)/shard_map/transpose | solution.py:85
  148.4 12.2 %reduce-scatter.7.cloned.1.call-done = f32[320,80]{1,0:T(8,128)} async-done(((f32[1280,80]{1,0:T(8,128)}), f32[320,80]{1,0:T(8,128)}) %reduce-scatter.7.cloned.1.call-update) | async-done | bytes 102416
  160.7 1.0 copy.25
  161.7 3.5 %convolution_bitcast_fusion = f32[5120,80]{0,1:T(8,128)S(1)} fusion(bf16[5120,320]{1,0:T(8,128)(2,1)} %bitcast.87, f32[80,320]{1,0:T(8,128)S(1)} %copy.25, bf16[80,320]{1,0:T(8,128)(2,1)S(1)} %copy-done.4), kind=kOutput, calls=%fused_computation.3 | convolution fusion | flops 262425600 | bytes 5068800 | tf_op jit(solution)/shard_map/dot_general | solution.py:89
  165.2 2.0 copy.26
  167.2 0.8 copy-done.2
  168.1 4.2 %collective-permute-start.1 = (bf16[2,320,80]{1,2,0:T(8,128)(2,1)S(1)}, bf16[2,320,80]{1,2,0:T(8,128)(2,1)S(1)}, u32[]{:S(2)}, u32[]{:S(2)}) collective-permute-start(bf16[2,320,80]{1,2,0:T(8,128)(2,1)S(1)} %pad_maximum_fusion.1), channel_id=1, source_target_pairs={{4,0},{8,4},{12,8},{16,12},{20,16},{24,20},{28,24},{32,28},{36,32}... | collective-permute-start | bytes 307208 | tf_op jit(solution)/shard_map/ppermute | solution.py:23
  172.3 3.1 %collective-permute-start = (bf16[2,320,80]{1,2,0:T(8,128)(2,1)S(1)}, bf16[2,320,80]{1,2,0:T(8,128)(2,1)S(1)}, u32[]{:S(2)}, u32[]{:S(2)}) collective-permute-start(bf16[2,320,80]{1,2,0:T(8,128)(2,1)S(1)} %pad_maximum_fusion.1), channel_id=1, source_target_pairs={{0,4},{4,8},{8,12},{12,16},{16,20},{20,24},{24,28},{28,32},{32,36}... | collective-permute-start | bytes 307208 | tf_op jit(solution)/shard_map/ppermute | solution.py:22
  176.7 0.6 collective-permute-done
  177.4 0.5 fusion.45
  177.9 0.4 fusion.6
  178.6 99.6 %reduce-scatter.9.cloned.1.call-done = f32[320,80]{1,0:T(8,128)} async-done(((f32[5120,80]{1,0:T(8,128)}), f32[320,80]{1,0:T(8,128)}) %reduce-scatter.9.cloned.1.call-update) | async-done | bytes 102416
  278.2 1.0 copy.27
  280.4 1.0 fusion.10
  281.8 5.5 %collective-permute-start.3 = (bf16[2,320,80]{1,2,0:T(8,128)(2,1)S(1)}, bf16[2,320,80]{1,2,0:T(8,128)(2,1)S(1)}, u32[]{:S(2)}, u32[]{:S(2)}) collective-permute-start(bf16[2,320,80]{1,2,0:T(8,128)(2,1)S(1)} %get-tuple-element.4), channel_id=1, source_target_pairs={{0,4},{4,8},{8,12},{12,16},{16,20},{20,24},{24,28},{28,32},{32,36}... | collective-permute-start | bytes 307208 | tf_op jit(solution)/shard_map/ppermute | solution.py:12
  287.3 1.9 collective-permute-start.2
  289.3 4.2 %collective-permute-done.2 = bf16[2,320,80]{1,2,0:T(8,128)(2,1)S(1)} collective-permute-done((bf16[2,320,80]{1,2,0:T(8,128)(2,1)S(1)}, bf16[2,320,80]{1,2,0:T(8,128)(2,1)S(1)}, u32[]{:S(2)}, u32[]{:S(2)}) %collective-permute-start.2) | collective-permute-done | bytes 102432 | tf_op jit(solution)/shard_map/ppermute | solution.py:12
  293.7 0.7 slice_bitcast_fusion.6
  (51 shorter events, 4.2 us)
Async XLA Ops:
  7.2 170.2 %copy-start = (bf16[320,80]{0,1:T(8,128)(2,1)S(1)}, bf16[320,80]{0,1:T(8,128)(2,1)}, u32[]{:S(2)}) copy-start(bf16[320,80]{0,1:T(8,128)(2,1)} %param.14) | copy-start | bytes 153604
  9.8 52.8 %all-to-all-start = ((s32[64,1,2]{2,1,0:T(1,128)}), s32[64,1,2]{2,1,0:T(1,128)S(1)}, u32[]{:S(2)}, u32[]{:S(2)}) async-start(s32[64,1,2]{2,1,0:T(1,128)} %bitcast.6), calls=%async_computation | async-start | bytes 65536 | tf_op jit(solution)/shard_map/all_to_all | solution.py:70
  62.6 70.1 %all-to-all-start.1 = ((bf16[64,2,2048]{2,1,0:T(2,128)(2,1)}), bf16[64,2,2048]{2,1,0:T(2,128)(2,1)S(1)}, u32[]{:S(2)}, u32[]{:S(2)}) async-start(bf16[64,2,2048]{2,1,0:T(2,128)(2,1)} %reshape.182), calls=%async_computation.1 | async-start | bytes 1048576 | tf_op jit(solution)/shard_map/all_to_all | solution.py:69
  68.3 92.4 %reduce-scatter.7.cloned.1.call-start = ((), (), s32[]{:S(2)}) async-start(), calls=%async_computation.4 | async-start | bytes 819200
  134.9 5.2 %copy-start.1 = (bf16[5120,320]{0,1:T(8,128)(2,1)S(1)}, bf16[5120,320]{0,1:T(8,128)(2,1)}, u32[]{:S(2)}) copy-start(bf16[5120,320]{0,1:T(8,128)(2,1)} %param.13) | copy-start | bytes 9830404
  140.1 138.1 %reduce-scatter.9.cloned.1.call-start = ((), (), s32[]{:S(2)}) async-start(), calls=%async_computation.5 | async-start | bytes 2785280
  143.8 17.9 %copy-start.4 = (bf16[80,320]{1,0:T(8,128)(2,1)S(1)}, bf16[80,320]{1,0:T(8,128)(2,1)}, u32[]{:S(2)}) copy-start(bf16[80,320]{1,0:T(8,128)(2,1)} %param.12) | copy-start | bytes 153604
  167.2 0.8 copy-start.2
  167.2 0.9 copy-start.3
  167.2 8.2 %copy-start.5 = (s32[192]{0:T(256)S(1)}, s32[192]{0:T(256)}, u32[]{:S(2)}) copy-start(s32[192]{0:T(256)} %param.17) | copy-start | bytes 2308
  168.1 8.6 %collective-permute-start.1 = (bf16[2,320,80]{1,2,0:T(8,128)(2,1)S(1)}, bf16[2,320,80]{1,2,0:T(8,128)(2,1)S(1)}, u32[]{:S(2)}, u32[]{:S(2)}) collective-permute-start(bf16[2,320,80]{1,2,0:T(8,128)(2,1)S(1)} %pad_maximum_fusion.1), channel_id=1, source_target_pairs={{4,0},{8,4},{12,8},{16,12},{20,16},{24,20},{28,24},{32,28},{36,32}... | collective-permute-start | bytes 307208 | tf_op jit(solution)/shard_map/ppermute | solution.py:23
  172.3 5.0 %collective-permute-start = (bf16[2,320,80]{1,2,0:T(8,128)(2,1)S(1)}, bf16[2,320,80]{1,2,0:T(8,128)(2,1)S(1)}, u32[]{:S(2)}, u32[]{:S(2)}) collective-permute-start(bf16[2,320,80]{1,2,0:T(8,128)(2,1)S(1)} %pad_maximum_fusion.1), channel_id=1, source_target_pairs={{0,4},{4,8},{8,12},{12,16},{16,20},{20,24},{24,28},{28,32},{32,36}... | collective-permute-start | bytes 307208 | tf_op jit(solution)/shard_map/ppermute | solution.py:22
  281.8 7.5 %collective-permute-start.3 = (bf16[2,320,80]{1,2,0:T(8,128)(2,1)S(1)}, bf16[2,320,80]{1,2,0:T(8,128)(2,1)S(1)}, u32[]{:S(2)}, u32[]{:S(2)}) collective-permute-start(bf16[2,320,80]{1,2,0:T(8,128)(2,1)S(1)} %get-tuple-element.4), channel_id=1, source_target_pairs={{0,4},{4,8},{8,12},{12,16},{16,20},{20,24},{24,28},{28,32},{32,36}... | collective-permute-start | bytes 307208 | tf_op jit(solution)/shard_map/ppermute | solution.py:12
  287.3 6.2 %collective-permute-start.2 = (bf16[2,320,80]{1,2,0:T(8,128)(2,1)S(1)}, bf16[2,320,80]{1,2,0:T(8,128)(2,1)S(1)}, u32[]{:S(2)}, u32[]{:S(2)}) collective-permute-start(bf16[2,320,80]{1,2,0:T(8,128)(2,1)S(1)} %get-tuple-element.3), channel_id=1, source_target_pairs={{4,0},{8,4},{12,8},{16,12},{20,16},{24,20},{28,24},{32,28},{36,32}... | collective-permute-start | bytes 307208 | tf_op jit(solution)/shard_map/ppermute | solution.py:12
Sparse Core Ops, SparseCore 0:
  140.2 20.4 reduce-scatter.6
  167.4 110.8 reduce-scatter.8
where the time goes:
time: 302 us; the launch traced here: 301 us
  waiting for transfers between devices  199 us (66%)
  starting transfers between devices  50.9 us (17%)
  local copies, waits for them, and re-layouts  22 us (7%)
  between operations  14.3 us (5%)
  matrix products  11.3 us (4%)
  other arithmetic  3.43 us (1%)
    unnamed x4, waiting for transfers between devices  112 us
    all_to_all x1, waiting for transfers between devices, on_device(): lax.all_to_all(packed, 'grp', split_axis=0, concat_axis=0, tiled=True)  62.9 us
    all_to_all x1, starting transfers between devices, on_device(): lax.all_to_all(labels, 'grp', split_axis=0, concat_axis=0, tiled=True)  30.4 us
    all_to_all x1, waiting for transfers between devices, on_device(): lax.all_to_all(labels, 'grp', split_axis=0, concat_axis=0, tiled=True)  19.5 us
    unnamed x16, local copies, waits for them, and re-layouts  8.6 us
    ppermute x2, starting transfers between devices, passed_along(): return lax.ppermute(block, axis, route)  7.45 us
  transfers between devices with their start and end apart: 8, of which 6 were waited for; matrix products, arithmetic and copies ran while one was open for 5% of the time, Pallas kernels for 0%

commit v1 on v0

--- a/solution.py
+++ b/solution.py
@@ -30,28 +30,16 @@
     return normal_cdf + values * jnp.exp(-0.5 * values * values) * 0.3989422804014327
 
 
-def pack_rows(rows, destination, groups):
-    row_count = rows.shape[0]
-    row_width = rows.shape[1]
+def packing(destination, groups, row_count):
     offsets = min(groups, row_count // 2)
     capacity = row_count // offsets
     targets = destination // row_count
     slot_ids = destination % row_count
-    matches = (targets[:, None] == jnp.arange(groups, dtype=jnp.int32)[None, :]).astype(jnp.int32)
-    send_order = jnp.sum((jnp.cumsum(matches, 0) - 1) * matches, 1)
-    buffer_index = targets * capacity + send_order
-    packed = jnp.zeros((groups * capacity, row_width), rows.dtype).at[buffer_index].set(rows)
-    labels = jnp.full((groups * capacity,), row_count, jnp.int32).at[buffer_index].set(slot_ids)
-    return (packed.reshape(groups, capacity, row_width), labels.reshape(groups, capacity))
-
-
-def unpack_rows(packed, labels, row_count):
-    row_width = packed.shape[2]
-    flattened = packed.reshape(-1, row_width)
-    placed = (
-        jnp.zeros((row_count + 1, row_width), packed.dtype).at[labels.reshape(-1)].set(flattened)
-    )
-    return placed[:row_count]
+    order = jnp.arange(row_count, dtype=jnp.int32)
+    earlier = (targets[:, None] == targets[None, :]) & (order[:, None] < order[None, :])
+    index = targets * capacity + jnp.sum(earlier.astype(jnp.int32), 0)
+    slots = jnp.arange(groups * capacity, dtype=jnp.int32)
+    return (index[None, :] == slots[:, None]).astype(jnp.bfloat16), slot_ids
 
 
 def send_back(terms, offset_by):
@@ -64,33 +52,41 @@
     groups = lax.axis_size("grp")
     merged_rows = grad_out.shape[0]
     contract_last = (((1,), (1,)), ((), ()))
-    packed, labels = pack_rows(grad_out, destination, groups)
-    arrived, arrived_ids = (
-        lax.all_to_all(packed, "grp", split_axis=0, concat_axis=0, tiled=True),
-        lax.all_to_all(labels, "grp", split_axis=0, concat_axis=0, tiled=True),
+    spans = lax.axis_size("span")
+    sects = lax.axis_size("sect")
+    local_hidden = w_up.shape[1]
+    partial_hidden = lax.dot_general(
+        grad_out, w_down, contract_last, preferred_element_type=jnp.float32
+    ).astype(jnp.bfloat16)
+    sent = partial_hidden.reshape(merged_rows, spans, local_hidden).transpose(1, 0, 2)
+    terms = lax.all_to_all(sent, "span", split_axis=0, concat_axis=0, tiled=True)
+    rows = jnp.sum(terms.astype(jnp.float32), 0).astype(jnp.bfloat16)
+    packer, slot_ids = packing(destination, groups, merged_rows)
+    labelled = jnp.concatenate(
+        [rows, (slot_ids + 1).astype(jnp.bfloat16)[:, None], jnp.zeros((merged_rows, 63), jnp.bfloat16)], 1
     )
-    grad_enc = unpack_rows(arrived, arrived_ids, merged_rows)
-    partial_hidden = lax.dot_general(
-        grad_enc, w_down, contract_last, preferred_element_type=jnp.float32
+    packed = jnp.dot(packer, labelled, preferred_element_type=jnp.float32).astype(jnp.bfloat16)
+    arrived = lax.all_to_all(packed, "grp", split_axis=0, concat_axis=0, tiled=True)
+    label = arrived[:, local_hidden].astype(jnp.int32)
+    unpacker = (
+        label[None, :] == jnp.arange(1, merged_rows + 1, dtype=jnp.int32)[:, None]
+    ).astype(jnp.bfloat16)
+    grad_hidden = jnp.dot(
+        unpacker, arrived[:, :local_hidden], preferred_element_type=jnp.float32
     )
-    grad_hidden = lax.psum_scatter(partial_hidden, "span", scatter_dimension=1, tiled=True)
     grad_pre = (grad_hidden * gelu_slope(pre_act.astype(jnp.float32))).astype(jnp.bfloat16)
-    head_devices = lax.axis_size(("sect", "span"))
+    head_devices = sects * spans
     merge_rows = w_up.shape[0]
-    local_hidden = w_up.shape[1]
     head_cols = queries.shape[1]
     heads_here = head_cols // HEAD_DIM
-    reordered = (
-        w_up.reshape(4, head_devices, head_cols, local_hidden)
-        .transpose(1, 0, 2, 3)
-        .reshape(merge_rows, local_hidden)
-    )
-    share = lax.psum_scatter(
-        lax.dot_general(reordered, grad_pre, contract_last, preferred_element_type=jnp.float32),
-        ("sect", "span"),
-        scatter_dimension=0,
-        tiled=True,
-    )
+    merged = lax.dot_general(
+        w_up, grad_pre, contract_last, preferred_element_type=jnp.float32
+    ).astype(jnp.bfloat16)
+    merged = merged.reshape(4, sects, spans, head_cols, merged_rows).transpose(1, 2, 0, 3, 4)
+    first = lax.all_to_all(merged, "sect", split_axis=0, concat_axis=0, tiled=True)
+    first = jnp.sum(first.astype(jnp.float32), 0).astype(jnp.bfloat16)
+    second = lax.all_to_all(first, "span", split_axis=0, concat_axis=0, tiled=True)
+    share = jnp.sum(second.astype(jnp.float32), 0)
     patches = 4 * merged_rows
     grad_attn = (
         share.reshape(4, head_cols, merged_rows)

time: 302 us -> 148 us (0.49)
  waiting for transfers between devices: 199 us -> 47.4 us
  between operations: 14.3 us -> 0.95 us
  other arithmetic: 3.43 us -> 13 us
  local copies, waits for them, and re-layouts: 22 us -> 14.2 us
  starting transfers between devices: 50.9 us -> 57.7 us
    unnamed x4 -> x0, waiting for transfers between devices: 112 us -> none
    all_to_all x1, waiting for transfers between devices: 62.9 us -> 27.3 us  [on_device(): lax.all_to_all(packed, 'grp', split_axis=0, concat_axis=0, tiled=True)]
    all_to_all x1 -> x3, starting transfers between devices: 30.4 us -> 11.9 us  [the longest x1 4.41 us: on_device(): lax.all_to_all(merged, 'sect', split_axis=0, concat_axis=0, tiled=True)]
    all_to_all x1, starting transfers between devices: 5.66 us -> 20.1 us  [on_device(): lax.all_to_all(packed, 'grp', split_axis=0, concat_axis=0, tiled=True)]
    ppermute x1, starting transfers between devices: 4.18 us -> 16.1 us  [extended(): after = lax.ppermute(first, axis, down)]
    unnamed x16 -> x22, local copies, waits for them, and re-layouts: 8.6 us -> 1.84 us
    reshape x4 -> x5, local copies, waits for them, and re-layouts: 1.47 us -> 8.19 us  [the longest x2 6.24 us: on_device(): merged.reshape(4, sects, spans, head_cols, merged_rows)]
    reduce_sum x1 -> x4, other arithmetic: 0.17 us -> 5.48 us  [the longest x1 3 us: on_device(): first = jnp.sum(first.astype(jnp.float32), 0).astype(jnp.bfloat16)]
  transfers between devices with their start and end apart: 8 -> 8, of which waited for: 6 -> 6; matrix products, arithmetic and copies ran while one was open for 5% -> 18% of each run, Pallas kernels for 0% -> 0%
where the time goes in v1:
time: 148 us; the launch traced here: 147 us
  starting transfers between devices  57.7 us (39%)
  waiting for transfers between devices  47.4 us (32%)
  local copies, waits for them, and re-layouts  14.2 us (10%)
  matrix products  13.8 us (9%)
  other arithmetic  13 us (9%)
    all_to_all x1, waiting for transfers between devices, on_device(): lax.all_to_all(packed, 'grp', split_axis=0, concat_axis=0, tiled=True)  27.3 us
    all_to_all x1, starting transfers between devices, on_device(): lax.all_to_all(packed, 'grp', split_axis=0, concat_axis=0, tiled=True)  20.1 us
    ppermute x1, starting transfers between devices, extended(): after = lax.ppermute(first, axis, down)  16.1 us
    all_to_all x1, waiting for transfers between devices, on_device(): lax.all_to_all(merged, 'sect', split_axis=0, concat_axis=0, tiled=True)  11.2 us
    ppermute x2, starting transfers between devices, passed_along(): return lax.ppermute(block, axis, route)  7.72 us
    reshape x2, local copies, waits for them, and re-layouts, on_device(): merged.reshape(4, sects, spans, head_cols, merged_rows)  6.24 us
    dot_general x1, matrix products, on_device(): lax.dot_general(grad_out, w_down, contract_last, preferred_element_type=j...  4.99 us
    all_to_all x1, starting transfers between devices, on_device(): lax.all_to_all(merged, 'sect', split_axis=0, concat_axis=0, tiled=True)  4.41 us
  transfers between devices with their start and end apart: 8, of which 6 were waited for; matrix products, arithmetic and copies ran while one was open for 18% of the time, Pallas kernels for 0%

profile of v1, /device:TPU:1, one launch (start us, length us, event | category | flops | bytes accessed | tf_op | source)
XLA Modules:
  0.0 147.1 jit_solution(12738080187606849749)
XLA Ops:
  0.6 1.7 %pad_maximum_fusion.1 = bf16[2,320,80]{1,2,0:T(8,128)(2,1)} fusion(bf16[1,320,80]{1,2,0:T(8,128)(2,1)} %bitcast.89, bf16[1,320,80]{1,2,0:T(8,128)(2,1)} %bitcast.91), kind=kLoop, calls=%fused_computation.46 | loop fusion | flops 51200 | bytes 204800 | tf_op jit(solution)/shard_map/stack | solution.py:97
  2.3 16.1 %collective-permute-start.1 = (bf16[2,320,80]{1,2,0:T(8,128)(2,1)}, bf16[2,320,80]{1,2,0:T(8,128)(2,1)}, u32[]{:S(2)}, u32[]{:S(2)}) collective-permute-start(bf16[2,320,80]{1,2,0:T(8,128)(2,1)} %pad_maximum_fusion.1), channel_id=1, source_target_pairs={{4,0},{8,4},{12,8},{16,12},{20,16},{24,20},{28,24},{32,28},{36,32}... | collective-permute-start | bytes 307208 | tf_op jit(solution)/shard_map/ppermute | solution.py:23
  18.4 1.9 %collective-permute-start = (bf16[2,320,80]{1,2,0:T(8,128)(2,1)}, bf16[2,320,80]{1,2,0:T(8,128)(2,1)}, u32[]{:S(2)}, u32[]{:S(2)}) collective-permute-start(bf16[2,320,80]{1,2,0:T(8,128)(2,1)} %pad_maximum_fusion.1), channel_id=1, source_target_pairs={{0,4},{4,8},{8,12},{12,16},{16,20},{20,24},{24,28},{28,32},{32,36}... | collective-permute-start | bytes 307208 | tf_op jit(solution)/shard_map/ppermute | solution.py:22
  20.3 5.0 %convolution_convert_fusion.1 = bf16[80,1280]{1,0:T(8,128)(2,1)} fusion(bf16[80,2048]{1,0:T(8,128)(2,1)} %param.9, bf16[1280,2048]{1,0:T(8,128)(2,1)} %param.11), kind=kOutput, calls=%fused_computation.2 | convolution fusion | flops 419532800 | bytes 5775360 | tf_op jit(solution)/shard_map/dot_general | solution.py:58
  25.3 1.2 reshape.149
  26.6 0.7 copy.39
  27.3 3.4 %all-to-all-start = ((bf16[4,80,320]{2,1,0:T(8,128)(2,1)}), bf16[4,80,320]{2,1,0:T(8,128)(2,1)S(1)}, u32[]{:S(2)}, u32[]{:S(2)}) async-start(bf16[4,80,320]{2,1,0:T(8,128)(2,1)} %bitcast.88), calls=%async_computation | async-start | bytes 491520 | tf_op jit(solution)/shard_map/all_to_all | solution.py:62
  31.5 0.7 multiply_add_fusion
  32.2 3.9 %all-to-all-done = bf16[4,80,320]{2,1,0:T(8,128)(2,1)S(1)} async-done(((bf16[4,80,320]{2,1,0:T(8,128)(2,1)}), bf16[4,80,320]{2,1,0:T(8,128)(2,1)S(1)}, u32[]{:S(2)}, u32[]{:S(2)}) %all-to-all-start) | async-done | bytes 204832 | tf_op jit(solution)/shard_map/all_to_all | solution.py:62
  36.8 1.0 convolution_convert_fusion.2
  38.5 20.1 %all-to-all-start.1 = ((bf16[64,2,384]{2,1,0:T(2,128)(2,1)}), bf16[64,2,384]{2,1,0:T(2,128)(2,1)S(1)}, u32[]{:S(2)}, u32[]{:S(2)}) async-start(bf16[64,2,384]{2,1,0:T(2,128)(2,1)} %all_to_all.18), calls=%async_computation.1 | async-start | bytes 196608 | tf_op jit(solution)/shard_map/all_to_all | solution.py:69
  59.4 27.3 %all-to-all-done.1 = bf16[64,2,384]{2,1,0:T(2,128)(2,1)S(1)} async-done(((bf16[64,2,384]{2,1,0:T(2,128)(2,1)}), bf16[64,2,384]{2,1,0:T(2,128)(2,1)S(1)}, u32[]{:S(2)}, u32[]{:S(2)}) %all-to-all-start.1) | async-done | bytes 98336 | tf_op jit(solution)/shard_map/all_to_all | solution.py:69
  86.9 2.7 %fusion = bf16[5120,80]{0,1:T(8,128)(2,1)} fusion(bf16[5120,320]{0,1:T(8,128)(2,1)S(1)} %copy-done, bf16[80,320]{1,0:T(8,128)(2,1)} %param.12, bf16[128,384]{1,0:T(8,128)(2,1)S(1)} %all_to_all.20, s32[128]{0:T(128)S(1)} %convert_reduce_fusion.1, s32[80]{0:T(128)S(1)} %iota_add_fusion.1), kind=kOutput, calls=%fused_computation.1 | convolution fusion | flops 269399040 | bytes 4246336 | tf_op jit(solution)/shard_map/dot_general | solution.py:82
  89.6 3.4 %reshape.150 = bf16[4,4,4,80,80]{3,2,1,0,4:T(4,128)(2,1)} reshape(bf16[5120,80]{0,1:T(8,128)(2,1)} %fusion) | data formatting | bytes 1638400 | tf_op jit(solution)/shard_map/reshape | solution.py:85
  93.0 2.9 %copy.38 = bf16[4,4,4,80,80]{3,2,0,4,1:T(4,128)(2,1)} copy(bf16[4,4,4,80,80]{3,2,1,0,4:T(4,128)(2,1)} %reshape.150) | data formatting | bytes 1638400 | tf_op jit(solution)/shard_map/reshape | solution.py:85
  95.9 4.4 %all-to-all-start.2 = ((bf16[4,4,4,80,80]{3,1,2,4,0:T(4,128)(2,1)}), bf16[4,4,4,80,80]{3,1,2,4,0:T(4,128)(2,1)}, u32[]{:S(2)}, u32[]{:S(2)}) async-start(bf16[4,4,4,80,80]{3,1,2,4,0:T(4,128)(2,1)} %bitcast.84), calls=%async_computation.2 | async-start | bytes 2621440 | tf_op jit(solution)/shard_map/all_to_all | solution.py:86
  100.8 1.1 pad_maximum_fusion
  101.9 0.7 copy-done.3
  102.6 1.3 fusion.56
  103.9 1.1 copy-done.2
  105.4 11.2 %all-to-all-done.2 = bf16[4,4,4,80,80]{3,1,2,4,0:T(4,128)(2,1)} async-done(((bf16[4,4,4,80,80]{3,1,2,4,0:T(4,128)(2,1)}), bf16[4,4,4,80,80]{3,1,2,4,0:T(4,128)(2,1)}, u32[]{:S(2)}, u32[]{:S(2)}) %all-to-all-start.2) | async-done | bytes 819232 | tf_op jit(solution)/shard_map/all_to_all | solution.py:86
  116.6 3.0 %reduce_sum.73 = bf16[4,4,80,80]{2,0,1,3:T(4,128)(2,1)} reduce(bf16[4,4,4,80,80]{3,1,2,4,0:T(4,128)(2,1)} %all-to-all-done.2, bf16[]{:T(256)} %constant.55.clone.1), dimensions={0}, to_apply=%region_7.8 | reduce | flops 307200 | bytes 1024002 | tf_op jit(solution)/shard_map/reduce_sum | solution.py:87
  119.6 1.8 %copy.33 = bf16[4,4,80,80]{2,1,3,0:T(4,128)(2,1)} copy(bf16[4,4,80,80]{2,0,1,3:T(4,128)(2,1)} %reduce_sum.73) | data formatting | bytes 409600 | tf_op jit(solution)/shard_map/reduce_sum | solution.py:87
  121.4 4.1 %all-to-all-start.3 = ((bf16[4,4,80,80]{2,1,3,0:T(4,128)(2,1)}), bf16[4,4,80,80]{2,1,3,0:T(4,128)(2,1)}, u32[]{:S(2)}, u32[]{:S(2)}) async-start(bf16[4,4,80,80]{2,1,3,0:T(4,128)(2,1)} %copy.33), calls=%async_computation.3 | async-start | bytes 655360 | tf_op jit(solution)/shard_map/all_to_all | solution.py:88
  125.5 2.7 %fusion.6 = f32[320,960]{1,0:T(8,128)} fusion(f32[320,960]{1,0:T(8,128)} %copy-done.2, f32[320]{0:T(512)S(1)} %fusion.7, f32[320]{0:T(512)S(1)} %get-tuple-element.9), kind=kLoop, calls=%fused_computation.14 | loop fusion | flops 614400 | bytes 2460160 | tf_op jit(solution)/shard_map/div | solution.py:120
  128.2 3.3 %all-to-all-done.3 = bf16[4,4,80,80]{2,1,3,0:T(4,128)(2,1)} async-done(((bf16[4,4,80,80]{2,1,3,0:T(4,128)(2,1)}), bf16[4,4,80,80]{2,1,3,0:T(4,128)(2,1)}, u32[]{:S(2)}, u32[]{:S(2)}) %all-to-all-start.3) | async-done | bytes 204832 | tf_op jit(solution)/shard_map/all_to_all | solution.py:88
  131.5 1.2 reduce.7
  132.8 1.9 %fusion.11 = f32[320]{0:T(512)S(1)} fusion(f32[320,1,80]{0,2,1:T(8,128)S(1)} %copy.34, f32[320,960]{1,0:T(8,128)} %fusion.6, bf16[2,960,80]{1,2,0:T(8,128)(2,1)} %copy-done.3), kind=kOutput, calls=%fused_computation.23 | convolution fusion | flops 49510080 | bytes 1578240 | tf_op jit(solution)/shard_map/hqk,khe->qhe/dot_general | solution.py:122
  135.3 1.0 fusion.12
  136.7 5.6 %collective-permute-start.2 = (bf16[2,320,80]{1,2,0:T(8,128)(2,1)S(1)}, bf16[2,320,80]{1,2,0:T(8,128)(2,1)S(1)}, u32[]{:S(2)}, u32[]{:S(2)}) collective-permute-start(bf16[2,320,80]{1,2,0:T(8,128)(2,1)S(1)} %get-tuple-element.3), channel_id=1, source_target_pairs={{4,0},{8,4},{12,8},{16,12},{20,16},{24,20},{28,24},{32,28},{36,32}... | collective-permute-start | bytes 307208 | tf_op jit(solution)/shard_map/ppermute | solution.py:12
  142.3 2.1 %collective-permute-start.3 = (bf16[2,320,80]{1,2,0:T(8,128)(2,1)S(1)}, bf16[2,320,80]{1,2,0:T(8,128)(2,1)S(1)}, u32[]{:S(2)}, u32[]{:S(2)}) collective-permute-start(bf16[2,320,80]{1,2,0:T(8,128)(2,1)S(1)} %get-tuple-element.4), channel_id=1, source_target_pairs={{0,4},{4,8},{8,12},{12,16},{16,20},{20,24},{24,28},{28,32},{32,36}... | collective-permute-start | bytes 307208 | tf_op jit(solution)/shard_map/ppermute | solution.py:12
  145.0 1.2 collective-permute-done.3
  (57 shorter events, 6.4 us)
Async XLA Ops:
  0.6 86.2 %copy-start = (bf16[5120,320]{0,1:T(8,128)(2,1)S(1)}, bf16[5120,320]{0,1:T(8,128)(2,1)}, u32[]{:S(2)}) copy-start(bf16[5120,320]{0,1:T(8,128)(2,1)} %param.13) | copy-start | bytes 9830404
  2.3 98.4 %collective-permute-start.1 = (bf16[2,320,80]{1,2,0:T(8,128)(2,1)}, bf16[2,320,80]{1,2,0:T(8,128)(2,1)}, u32[]{:S(2)}, u32[]{:S(2)}) collective-permute-start(bf16[2,320,80]{1,2,0:T(8,128)(2,1)} %pad_maximum_fusion.1), channel_id=1, source_target_pairs={{4,0},{8,4},{12,8},{16,12},{20,16},{24,20},{28,24},{32,28},{36,32}... | collective-permute-start | bytes 307208 | tf_op jit(solution)/shard_map/ppermute | solution.py:23
  18.4 82.4 %collective-permute-start = (bf16[2,320,80]{1,2,0:T(8,128)(2,1)}, bf16[2,320,80]{1,2,0:T(8,128)(2,1)}, u32[]{:S(2)}, u32[]{:S(2)}) collective-permute-start(bf16[2,320,80]{1,2,0:T(8,128)(2,1)} %pad_maximum_fusion.1), channel_id=1, source_target_pairs={{0,4},{4,8},{8,12},{12,16},{16,20},{20,24},{24,28},{28,32},{32,36}... | collective-permute-start | bytes 307208 | tf_op jit(solution)/shard_map/ppermute | solution.py:22
  25.3 5.4 %copy-start.9 = (s32[80]{0:T(128)S(1)}, s32[80]{0:T(128)}, u32[]{:S(2)}) copy-start(s32[80]{0:T(128)} %param.10) | copy-start | bytes 964
  25.3 33.3 %copy-start.8 = (s32[192]{0:T(256)S(1)}, s32[192]{0:T(256)}, u32[]{:S(2)}) copy-start(s32[192]{0:T(256)} %param.17) | copy-start | bytes 2308
  27.3 8.8 %all-to-all-start = ((bf16[4,80,320]{2,1,0:T(8,128)(2,1)}), bf16[4,80,320]{2,1,0:T(8,128)(2,1)S(1)}, u32[]{:S(2)}, u32[]{:S(2)}) async-start(bf16[4,80,320]{2,1,0:T(8,128)(2,1)} %bitcast.88), calls=%async_computation | async-start | bytes 491520 | tf_op jit(solution)/shard_map/all_to_all | solution.py:62
  30.7 0.6 copy-start.10
  38.5 48.2 %all-to-all-start.1 = ((bf16[64,2,384]{2,1,0:T(2,128)(2,1)}), bf16[64,2,384]{2,1,0:T(2,128)(2,1)S(1)}, u32[]{:S(2)}, u32[]{:S(2)}) async-start(bf16[64,2,384]{2,1,0:T(2,128)(2,1)} %all_to_all.18), calls=%async_computation.1 | async-start | bytes 196608 | tf_op jit(solution)/shard_map/all_to_all | solution.py:69
  95.8 4.9 %copy-start.5 = (bf16[320,80]{0,1:T(8,128)(2,1)S(1)}, bf16[320,80]{0,1:T(8,128)(2,1)}, u32[]{:S(2)}) copy-start(bf16[320,80]{0,1:T(8,128)(2,1)} %param.16) | copy-start | bytes 153604
  95.9 4.9 %copy-start.6 = (bf16[320,80]{0,1:T(8,128)(2,1)S(1)}, bf16[320,80]{0,1:T(8,128)(2,1)}, u32[]{:S(2)}) copy-start(bf16[320,80]{0,1:T(8,128)(2,1)} %param.15) | copy-start | bytes 153604
  95.9 20.8 %all-to-all-start.2 = ((bf16[4,4,4,80,80]{3,1,2,4,0:T(4,128)(2,1)}), bf16[4,4,4,80,80]{3,1,2,4,0:T(4,128)(2,1)}, u32[]{:S(2)}, u32[]{:S(2)}) async-start(bf16[4,4,4,80,80]{3,1,2,4,0:T(4,128)(2,1)} %bitcast.84), calls=%async_computation.2 | async-start | bytes 2621440 | tf_op jit(solution)/shard_map/all_to_all | solution.py:86
  101.9 0.7 copy-start.3
  103.9 1.1 copy-start.2
  121.4 10.0 %all-to-all-start.3 = ((bf16[4,4,80,80]{2,1,3,0:T(4,128)(2,1)}), bf16[4,4,80,80]{2,1,3,0:T(4,128)(2,1)}, u32[]{:S(2)}, u32[]{:S(2)}) async-start(bf16[4,4,80,80]{2,1,3,0:T(4,128)(2,1)} %copy.33), calls=%async_computation.3 | async-start | bytes 655360 | tf_op jit(solution)/shard_map/all_to_all | solution.py:88
  132.8 1.9 %copy-start.1 = (f32[320,960]{1,0:T(8,128)S(1)}, f32[320,960]{1,0:T(8,128)}, u32[]{:S(2)}) copy-start(f32[320,960]{1,0:T(8,128)} %fusion.6) | copy-start | bytes 3686404
  132.8 2.2 %copy-start.4 = (bf16[2,960,80]{1,2,0:T(8,128)(2,1)S(1)}, bf16[2,960,80]{1,2,0:T(8,128)(2,1)}, u32[]{:S(2)}) copy-start(bf16[2,960,80]{1,2,0:T(8,128)(2,1)} %copy-done.3) | copy-start | bytes 921604
  135.0 1.3 copy-start.7
  136.7 8.4 %collective-permute-start.2 = (bf16[2,320,80]{1,2,0:T(8,128)(2,1)S(1)}, bf16[2,320,80]{1,2,0:T(8,128)(2,1)S(1)}, u32[]{:S(2)}, u32[]{:S(2)}) collective-permute-start(bf16[2,320,80]{1,2,0:T(8,128)(2,1)S(1)} %get-tuple-element.3), channel_id=1, source_target_pairs={{4,0},{8,4},{12,8},{16,12},{20,16},{24,20},{28,24},{32,28},{36,32}... | collective-permute-start | bytes 307208 | tf_op jit(solution)/shard_map/ppermute | solution.py:12
  142.3 3.9 %collective-permute-start.3 = (bf16[2,320,80]{1,2,0:T(8,128)(2,1)S(1)}, bf16[2,320,80]{1,2,0:T(8,128)(2,1)S(1)}, u32[]{:S(2)}, u32[]{:S(2)}) collective-permute-start(bf16[2,320,80]{1,2,0:T(8,128)(2,1)S(1)} %get-tuple-element.4), channel_id=1, source_target_pairs={{0,4},{4,8},{8,12},{12,16},{16,20},{20,24},{24,28},{28,32},{32,36}... | collective-permute-start | bytes 307208 | tf_op jit(solution)/shard_map/ppermute | solution.py:12

commit v2 on v1

v2 whole, which is shorter than its diff:
```python
import functools

import jax
import jax.numpy as jnp
from jax import lax
from jax.experimental import pallas as pl
from jax.experimental.pallas import tpu as pltpu
from jax.sharding import PartitionSpec as P

HEAD_DIM = 80
LABEL_LANES = 64
BF16 = jnp.bfloat16
F32 = jnp.float32
LAST = (((1,), (1,)), ((), ()))
FIRST = (((0,), (0,)), ((), ()))


def dot(a, b, dims=(((1,), (0,)), ((), ()))):
    return lax.dot_general(a, b, dims, preferred_element_type=F32)


def iota(shape, dim):
    return lax.broadcasted_iota(jnp.int32, shape, dim)


def gelu_slope(values):
    normal_cdf = 0.5 * (1.0 + lax.erf(values * 0.7071067811865476))
    return normal_cdf + values * jnp.exp(-0.5 * values * values) * 0.3989422804014327


def far_first(n):
    return sorted(range(1, n), key=lambda d: -min(d, n - d))


def token_packing(dest, rows, near, far, cap):
    where_to = dest.astype(F32)
    group = jnp.floor((where_to + 0.5) * (1.0 / rows))
    place = where_to - group * rows
    square = (rows, rows)
    across = jnp.broadcast_to(group, square)
    down = jnp.sum(jnp.where(iota(square, 0) == iota(square, 1), across, 0.0), 1, keepdims=True)
    earlier = (down == across) & (iota(square, 0) < iota(square, 1))
    copy = jnp.sum(jnp.where(earlier, 1.0, 0.0), 0, keepdims=True)
    group_hi = jnp.floor((group + 0.5) * (1.0 / near))
    slot = (group - group_hi * near) * (far * cap) + group_hi * cap + copy
    slots = near * far * cap
    hit = iota((slots, rows), 0).astype(F32) == slot
    label = jnp.sum(jnp.where(hit, place + 1.0, 0.0), 1, keepdims=True)
    return jnp.where(hit, 1.0, 0.0).astype(BF16), label


def image_ids(lengths, group, rows, tokens):
    images = lengths.shape[1]
    square = (images, images)
    sizes = jnp.broadcast_to(lengths.astype(F32), square)
    row, col = iota(square, 0), iota(square, 1)
    sizes_down = jnp.sum(jnp.where(row == col, sizes, 0.0), 1, keepdims=True)
    ends_down = jnp.sum(jnp.where(col <= row, sizes, 0.0), 1, keepdims=True)
    ends_across = jnp.sum(jnp.where(row <= col, sizes_down, 0.0), 0, keepdims=True)
    base = group * rows
    own = (base + (iota((4 * rows, 1), 0) >> 2)).astype(F32)
    near = (base - rows + (iota((1, 12 * rows), 1) >> 2)).astype(F32)
    own_image = jnp.sum(jnp.where(ends_across <= own, 1.0, 0.0), 1, keepdims=True)
    near_image = jnp.sum(jnp.where(ends_down <= near, 1.0, 0.0), 0, keepdims=True)
    inside = (near >= 0.0) & (near < float(tokens))
    return own_image, jnp.where(inside, near_image, -1.0)


def kernel(
    sizes,
    grad_out,
    dest,
    w_down,
    pre_act,
    w_up,
    queries,
    keys,
    values,
    lengths,
    out_q,
    out_k,
    out_v,
    go,
    wd,
    wu,
    pre,
    qs,
    kx,
    vx,
    dst,
    lens,
    part,
    part_in,
    near_out,
    near_in,
    far_out,
    far_in,
    mix,
    mix_a,
    mix_b,
    fin_a,
    fin_b,
    sum_a,
    sum_b,
    back,
    back_in,
    probs,
    load_sem,
    down_sem,
    part_s,
    part_r,
    halo_s,
    halo_r,
    near_s,
    near_r,
    far_s,
    far_r,
    a1_s,
    a1_r,
    b1_s,
    b1_r,
    a2_s,
    a2_r,
    b2_s,
    b2_r,
    back_s,
    back_r,
):
    sects, groups, spans, near, far, cap, split = sizes
    rows = grad_out.shape[0]
    hidden = w_up.shape[1]
    cols = queries.shape[1]
    patches = 4 * rows
    x, g, y = lax.axis_index("sect"), lax.axis_index("grp"), lax.axis_index("span")
    g_hi, g_lo = g // near, g % near

    def at_x(d):
        return ((x + d) % sects, g, y)

    def at_y(d):
        return (x, g, (y + d) % spans)

    def at_near(d):
        return (x, g_hi * near + (g_lo + d) % near, y)

    def at_far(d):
        return (x, ((g_hi + d) % far) * near + g_lo, y)

    def at_g(d):
        return (x, (g + d + groups) % groups, y)

    barrier = pltpu.get_barrier_semaphore()
    peers = [at_far(d) for d in far_first(far)]
    peers += [at_y(d) for d in range(1, spans)]
    peers += [at_near(d) for d in range(1, near)]
    peers += [at_g(1), at_g(-1)]
    peers += [at_x(d) for d in range(1, sects)]
    for peer in peers:
        pl.semaphore_signal(barrier, inc=1, device_id=peer, device_id_type=pl.DeviceIdType.MESH)

    sent = []

    def send(src, to, send_sem, recv_sem, peer):
        copy = pltpu.make_async_remote_copy(
            src_ref=src,
            dst_ref=to,
            send_sem=send_sem,
            recv_sem=recv_sem,
            device_id=peer,
            device_id_type=pl.DeviceIdType.MESH,
        )
        copy.start()
        sent.append(copy)
        return copy

    def load(src, to, sem):
        copy = pltpu.make_async_copy(src, to, sem)
        copy.start()
        return copy

    order_y = far_first(spans) + [0]
    load_go = load(grad_out, go, load_sem.at[0])
    load_dst = load(dest, dst, load_sem.at[1])
    load_wd = []
    for d in order_y:
        chunk = pl.ds(pl.multiple_of(((y + d) % spans) * hidden, 16), hidden)
        load_wd.append(load(w_down.at[chunk, :], wd.at[chunk, :], down_sem.at[d]))
    load_len = load(lengths, lens, load_sem.at[2])
    load_q = load(queries, qs, load_sem.at[3])
    load_k = load(keys, kx.at[pl.ds(patches, patches), :], load_sem.at[4])
    load_v = load(values, vx.at[pl.ds(patches, patches), :], load_sem.at[5])
    load_pre = load(pre_act, pre, load_sem.at[6])
    head_devices = sects * spans
    for d in range(head_devices):
        for p in range(4):
            load(
                w_up.at[pl.ds((p * head_devices + d) * cols, cols), :],
                wu.at[pl.ds((d * 4 + p) * cols, cols), :],
                load_sem.at[7],
            )

    load_dst.wait()
    packer, label = token_packing(dst[...], rows, near, far, cap)
    load_go.wait()
    own_part = None
    for d, loaded in zip(order_y, load_wd):
        loaded.wait()
        chunk = pl.ds(pl.multiple_of(((y + d) % spans) * hidden, 16), hidden)
        product = dot(go[...], wd[chunk, :], LAST)
        if d == 0:
            own_part = product
        else:
            part[d - 1] = product.astype(BF16)
    load_len.wait()
    own_image, near_image = image_ids(lens[...], g, rows, rows * groups)
    load_k.wait()
    load_v.wait()

    pl.semaphore_wait(barrier, len(peers))
    part_copies = [
        send(part.at[d - 1], part_in.at[d - 1], part_s.at[d - 1], part_r.at[d - 1], at_y(d))
        for d in far_first(spans)
    ]
    own_block = pl.ds(patches, patches)
    halo_copies = []
    for i, (full, step) in enumerate(((kx, 1), (vx, 1), (kx, -1), (vx, -1))):
        land = pl.ds(0 if step == 1 else 2 * patches, patches)
        halo_copies.append(
            send(full.at[own_block, :], full.at[land, :], halo_s.at[i], halo_r.at[i], at_g(step))
        )

    total = own_part
    for d, copy in zip(far_first(spans), part_copies):
        copy.wait_recv()
        total = total + part_in[d - 1].astype(F32)
    slots = near * far * cap
    near_rows, far_rows = far * cap, near * cap
    near_out[:, :hidden] = dot(packer, total.astype(BF16)).astype(BF16)
    near_out[:, hidden:] = jnp.broadcast_to(label, (slots, LABEL_LANES)).astype(BF16)
    near_copies = []
    for d in range(near - 1, 0, -1):
        block = pl.ds(pl.multiple_of(((g_lo + d) % near) * near_rows, near_rows), near_rows)
        near_copies.append(
            send(
                near_out.at[block, :],
                near_in.at[pl.ds(d * near_rows, near_rows), :],
                near_s.at[d - 1],
                near_r.at[d - 1],
                at_near(d),
            )
        )
    mine = pl.ds(pl.multiple_of(g_lo * near_rows, near_rows), near_rows)
    near_in[pl.ds(0, near_rows), :] = near_out[mine, :]
    out_row = iota((slots, slots), 0)
    in_row = iota((slots, slots), 1)
    source = ((out_row // cap) % near) * near_rows + (out_row // far_rows) * cap + out_row % cap
    shuffle = jnp.where(source == in_row, 1.0, 0.0).astype(BF16)
    for copy in near_copies:
        copy.wait_recv()
    far_out[...] = dot(shuffle, near_in[...]).astype(BF16)
    far_copies = []
    for d in far_first(far):
        block = pl.ds(pl.multiple_of(((g_hi + d) % far) * far_rows, far_rows), far_rows)
        far_copies.append(
            send(
                far_out.at[block, :],
                far_in.at[pl.ds(d * far_rows, far_rows), :],
                far_s.at[d - 1],
                far_r.at[d - 1],
                at_far(d),
            )
        )
    mine = pl.ds(pl.multiple_of(g_hi * far_rows, far_rows), far_rows)
    far_in[pl.ds(0, far_rows), :] = far_out[mine, :]

    scale = HEAD_DIM ** (-0.5)
    load_q.wait()
    for copy in halo_copies:
        copy.wait_recv()
    scores = dot(qs[...], kx[...], LAST) * scale
    scores = jnp.where(own_image == near_image, scores, -jnp.inf)
    top_score = jnp.max(scores, 1, keepdims=True)
    weights = jnp.exp(scores - top_score)
    probs[...] = weights / jnp.sum(weights, 1, keepdims=True)
    attended = dot(probs[...].astype(BF16), vx[...])
    load_pre.wait()
    slope = gelu_slope(pre[...].astype(F32))
    pltpu.make_async_copy(w_up, wu, load_sem.at[7]).wait()

    for copy in far_copies:
        copy.wait_recv()
    arrived = far_in[...]
    place = arrived[:, hidden : hidden + 1].astype(F32)
    unpacker = jnp.where(place == (iota((slots, rows), 1) + 1).astype(F32), 1.0, 0.0)
    grad_hidden = dot(unpacker.astype(BF16), arrived[:, :hidden], FIRST)
    grad_pre = (grad_hidden * slope).astype(BF16)
    top, low = pl.ds(0, split), pl.ds(split, rows - split)
    width = 4 * cols
    a_copies, b_copies = {}, {}
    for dx in far_first(sects) + [0]:
        for dy in far_first(spans) + [0]:
            owner = ((x + dx) % sects) * spans + (y + dy) % spans
            weight = wu[pl.ds(pl.multiple_of(owner * width, 16), width), :]
            mix[dx, dy] = dot(grad_pre, weight, LAST).astype(BF16)
            if dx:
                a_copies[dx, dy] = send(
                    mix.at[dx, dy, top, :],
                    mix_a.at[dx - 1, dy],
                    a1_s.at[dx - 1, dy],
                    a1_r.at[dx - 1, dy],
                    at_x(dx),
                )
            if dy:
                b_copies[dx, dy] = send(
                    mix.at[dx, dy, low, :],
                    mix_b.at[dy - 1, dx],
                    b1_s.at[dy - 1, dx],
                    b1_r.at[dy - 1, dx],
                    at_y(dy),
                )
    a2_copies, b2_copies = [], []
    share_a = share_b = None
    for dy in far_first(spans) + [0]:
        total = mix[0, dy, top, :].astype(F32)
        for dx in far_first(sects):
            a_copies[dx, dy].wait_recv()
            total = total + mix_a[dx - 1, dy].astype(F32)
        if dy:
            sum_a[dy - 1] = total.astype(BF16)
            a2_copies.append(
                send(sum_a.at[dy - 1], fin_a.at[dy - 1], a2_s.at[dy - 1], a2_r.at[dy - 1], at_y(dy))
            )
        else:
            share_a = total
    for dx in far_first(sects) + [0]:
        total = mix[dx, 0, low, :].astype(F32)
        for dy in far_first(spans):
            b_copies[dx, dy].wait_recv()
            total = total + mix_b[dy - 1, dx].astype(F32)
        if dx:
            sum_b[dx - 1] = total.astype(BF16)
            b2_copies.append(
                send(sum_b.at[dx - 1], fin_b.at[dx - 1], b2_s.at[dx - 1], b2_r.at[dx - 1], at_x(dx))
            )
        else:
            share_b = total
    for copy in a2_copies + b2_copies:
        copy.wait_recv()
    for d in range(spans - 1):
        share_a = share_a + fin_a[d].astype(F32)
    for d in range(sects - 1):
        share_b = share_b + fin_b[d].astype(F32)
    share = jnp.concatenate([share_a, share_b], 0).astype(BF16)

    patch_row, token = iota((patches, rows), 0), iota((patches, rows), 1)
    grad_attn = jnp.zeros((patches, cols), F32)
    for p in range(4):
        spread = jnp.where(patch_row == 4 * token + p, 1.0, 0.0).astype(BF16)
        grad_attn = grad_attn + dot(spread, share[:, p * cols : (p + 1) * cols])
    row_delta = jnp.sum(grad_attn.astype(BF16).astype(F32) * attended, 1, keepdims=True)
    grad_attn = grad_attn.astype(BF16)
    grad_scores = []
    back_copies = []
    q = qs[...]
    kept = None
    for block in (0, 2, 1):
        lanes = pl.ds(block * patches, patches)
        weights = probs[:, lanes]
        grad_probs = dot(grad_attn, vx[lanes, :], LAST)
        score_part = (weights * (grad_probs - row_delta)).astype(BF16)
        value_part = dot(weights.astype(BF16), grad_attn, FIRST)
        key_part = dot(score_part, q, FIRST) * scale
        grad_scores.append((lanes, score_part))
        if block == 1:
            kept = key_part, value_part
        else:
            side = block // 2
            back[side, 0] = key_part.astype(BF16)
            back[side, 1] = value_part.astype(BF16)
            back_copies.append(
                send(
                    back.at[side],
                    back_in.at[1 - side],
                    back_s.at[side],
                    back_r.at[1 - side],
                    at_g(block - 1),
                )
            )
    grad_query = jnp.zeros((patches, cols), F32)
    for lanes, score_part in grad_scores:
        grad_query = grad_query + dot(score_part, kx[lanes, :])
    out_q[...] = (grad_query * scale).astype(BF16)
    key_part, value_part = kept
    for copy in back_copies:
        copy.wait_recv()
    for side in range(2):
        key_part = key_part + back_in[side, 0].astype(F32)
        value_part = value_part + back_in[side, 1].astype(F32)
    out_k[...] = key_part.astype(BF16)
    out_v[...] = value_part.astype(BF16)
    for copy in sent:
        copy.wait_send()


def on_device(
    grad_out, destination, w_down, pre_act, w_up, queries, key_states, value_states, lengths
):
    sects, groups, spans = (lax.axis_size(a) for a in ("sect", "grp", "span"))
    rows, merged = grad_out.shape
    merge_rows, hidden = w_up.shape
    cols = queries.shape[1]
    patches = 4 * rows
    near = 8 if groups % 8 == 0 and groups > 8 else 2
    far = groups // near
    cap = rows // min(groups, rows // 2)
    slots = groups * cap
    split = (rows * 5 // 8 // 16) * 16 if rows >= 32 else rows // 2
    width = 4 * cols
    wide = hidden + LABEL_LANES
    dma = pltpu.SemaphoreType.DMA
    vmem = pltpu.VMEM
    some = pl.BlockSpec(memory_space=pl.ANY)
    out = jax.ShapeDtypeStruct((patches, cols), BF16)
    sizes = (sects, groups, spans, near, far, cap, split)
    return pl.pallas_call(
        functools.partial(kernel, sizes),
        out_shape=(out, out, out),
        in_specs=[some] * 9,
        out_specs=[pl.BlockSpec(memory_space=pltpu.VMEM)] * 3,
        scratch_shapes=[
            vmem((rows, merged), BF16),
            vmem(w_down.shape, BF16),
            vmem((merge_rows, hidden), BF16),
            vmem((rows, hidden), BF16),
            vmem((patches, cols), BF16),
            vmem((3 * patches, cols), BF16),
            vmem((3 * patches, cols), BF16),
            vmem((1, rows), jnp.int32),
            vmem((1, lengths.shape[0]), jnp.int32),
            vmem((spans - 1, rows, hidden), BF16),
            vmem((spans - 1, rows, hidden), BF16),
            vmem((slots, wide), BF16),
            vmem((slots, wide), BF16),
            vmem((slots, wide), BF16),
            vmem((slots, wide), BF16),
            vmem((sects, spans, rows, width), BF16),
            vmem((sects - 1, spans, split, width), BF16),
            vmem((spans - 1, sects, rows - split, width), BF16),
            vmem((spans - 1, split, width), BF16),
            vmem((sects - 1, rows - split, width), BF16),
            vmem((spans - 1, split, width), BF16),
            vmem((sects - 1, rows - split, width), BF16),
            vmem((2, 2, patches, cols), BF16),
            vmem((2, 2, patches, cols), BF16),
            vmem((patches, 3 * patches), F32),
            dma((8,)),
            dma((spans,)),
            dma((spans - 1,)),
            dma((spans - 1,)),
            dma((4,)),
            dma((4,)),
            dma((near - 1,)),
            dma((near - 1,)),
            dma((far - 1,)),
            dma((far - 1,)),
            dma((sects - 1, spans)),
            dma((sects - 1, spans)),
            dma((spans - 1, sects)),
            dma((spans - 1, sects)),
            dma((spans - 1,)),
            dma((spans - 1,)),
            dma((sects - 1,)),
            dma((sects - 1,)),
            dma((2,)),
            dma((2,)),
        ],
        compiler_params=pltpu.CompilerParams(
            collective_id=0, has_side_effects=True, vmem_limit_bytes=60 * 1024 * 1024
        ),
        name="merger_attention_backward",
    )(
        grad_out,
        destination.reshape(1, rows),
        w_down,
        pre_act,
        w_up,
        queries,
        key_states,
        value_states,
        lengths.reshape(1, lengths.shape[0]),
    )


def solution(mesh):
    placed = (
        P("grp", "span"),
        P("grp"),
        P("sect", "span"),
        P("grp", ("sect", "span")),
        P(None, ("sect", "span")),
        P("grp", ("sect", "span")),
        P("grp", ("sect", "span")),
        P("grp", ("sect", "span")),
        P(),
    )
    return jax.shard_map(
        on_device,
        mesh=mesh,
        in_specs=placed,
        out_specs=(
            P("grp", ("sect", "span")),
            P("grp", ("sect", "span")),
            P("grp", ("sect", "span")),
        ),
        check_vma=False,
    )
```

time: 148 us -> 88.6 us (0.60)
  Pallas kernels: 0 us -> 72.1 us
  starting transfers between devices: 57.7 us -> 0 us
  waiting for transfers between devices: 47.4 us -> 0 us
  matrix products: 13.8 us -> 0 us
  other arithmetic: 13 us -> 0 us
    pallas_call x0 -> x1, Pallas kernels: none -> 72.1 us  [on_device(): pl.pallas_call(functools.partial(kernel, sizes), out_shape=(out, out, out...]
    all_to_all x4 -> x0, waiting for transfers between devices: 45.7 us -> none  [the longest x1 27.3 us: on_device(): lax.all_to_all(packed, 'grp', split_axis=0, concat_axis=0, tiled=True)]
    all_to_all x4 -> x0, starting transfers between devices: 32 us -> none  [the longest x1 20.1 us: on_device(): lax.all_to_all(packed, 'grp', split_axis=0, concat_axis=0, tiled=True)]
    ppermute x4 -> x0, starting transfers between devices: 25.7 us -> none  [the longest x1 16.1 us: extended(): after = lax.ppermute(first, axis, down)]
    dot_general x9 -> x0, matrix products: 13.8 us -> none  [the longest x1 4.99 us: on_device(): lax.dot_general(grad_out, w_down, contract_last, preferred_element_type=j...]
    unnamed x22 -> x4, local copies, waits for them, and re-layouts: 1.84 us -> 10.5 us
    reshape x5 -> x0, local copies, waits for them, and re-layouts: 8.19 us -> none  [the longest x2 6.24 us: on_device(): merged.reshape(4, sects, spans, head_cols, merged_rows)]
    reduce_sum x6 -> x0, other arithmetic: 5.94 us -> none  [the longest x1 3 us: on_device(): first = jnp.sum(first.astype(jnp.float32), 0).astype(jnp.bfloat16)]
  transfers between devices with their start and end apart: 8 -> 0, of which waited for: 6 -> 0; matrix products, arithmetic and copies ran while one was open for 18% -> 0% of each run, Pallas kernels for 0% -> 0%
where the time goes in v2:
time: 88.6 us; the launch traced here: 88.1 us
  Pallas kernels  72.1 us (81%)
  local copies, waits for them, and re-layouts  15.3 us (17%)
    pallas_call x1, Pallas kernels, on_device(): pl.pallas_call(functools.partial(kernel, sizes), out_shape=(out, out, out...  72.1 us
    unnamed x4, local copies, waits for them, and re-layouts  10.5 us
    pallas_call x3, local copies, waits for them, and re-layouts, on_device(): pl.pallas_call(functools.partial(kernel, sizes), out_shape=(out, out, out...  4.81 us

profile of v2, /device:TPU:1, one launch (start us, length us, event | category | flops | bytes accessed | tf_op | source)
XLA Modules:
  0.0 88.1 jit_solution(706225626258177777)
XLA Ops:
  0.6 1.6 %copy.13.queries = bf16[320,80]{1,0:T(8,128)(2,1)} copy(bf16[320,80]{0,1:T(8,128)(2,1)} %param.14) | data formatting | bytes 102400 | tf_op args[5]
  2.2 1.6 %copy.14.keys = bf16[320,80]{1,0:T(8,128)(2,1)} copy(bf16[320,80]{0,1:T(8,128)(2,1)} %param.15) | data formatting | bytes 102400 | tf_op args[6]
  3.8 1.6 %copy.15.values = bf16[320,80]{1,0:T(8,128)(2,1)} copy(bf16[320,80]{0,1:T(8,128)(2,1)} %param.16) | data formatting | bytes 102400 | tf_op args[7]
  5.3 5.8 %copy.12.w_up = bf16[5120,320]{1,0:T(8,128)(2,1)} copy(bf16[5120,320]{0,1:T(8,128)(2,1)} %param.13) | data formatting | bytes 6553600 | tf_op args[4]
  11.1 72.1 %merger_attention_backward.1 = (bf16[320,80]{1,0:T(8,128)(2,1)}, bf16[320,80]{1,0:T(8,128)(2,1)}, bf16[320,80]{1,0:T(8,128)(2,1)}) custom-call(bf16[80,2048]{1,0:T(8,128)(2,1)} %grad_out.1, s32[1,80]{1,0:T(1,128)} %bitcast.3, bf16[1280,2048]{1,0:T(8,128)(2,1)} %w_down.1, bf16[80,320]{1,0:T(8,128)(2,1)} %pre_act.1, bf16[5120,320]{1,0:T(8,128)(2,1)} %copy.12.w_up, ...), custom_call_target="tpu_custom_call" | custom-call | tf_op jit(solution)/shard_map/merger_attention_backward/pallas_call | solution.py:425
  83.3 1.6 %copy.16 = bf16[320,80]{0,1:T(8,128)(2,1)} copy(bf16[320,80]{1,0:T(8,128)(2,1)} %get-tuple-element.3) | data formatting | bytes 102400 | tf_op jit(solution)/shard_map/merger_attention_backward/pallas_call | solution.py:425
  84.9 1.6 %copy.17 = bf16[320,80]{0,1:T(8,128)(2,1)} copy(bf16[320,80]{1,0:T(8,128)(2,1)} %get-tuple-element.4) | data formatting | bytes 102400 | tf_op jit(solution)/shard_map/merger_attention_backward/pallas_call | solution.py:425
  86.5 1.6 %copy.18 = bf16[320,80]{0,1:T(8,128)(2,1)} copy(bf16[320,80]{1,0:T(8,128)(2,1)} %get-tuple-element.5) | data formatting | bytes 102400 | tf_op jit(solution)/shard_map/merger_attention_backward/pallas_call | solution.py:425

commit v3 on v2

--- a/solution.py
+++ b/solution.py
@@ -58,10 +58,10 @@
     ends_down = jnp.sum(jnp.where(col <= row, sizes, 0.0), 1, keepdims=True)
     ends_across = jnp.sum(jnp.where(row <= col, sizes_down, 0.0), 0, keepdims=True)
     base = group * rows
-    own = (base + (iota((4 * rows, 1), 0) >> 2)).astype(F32)
-    near = (base - rows + (iota((1, 12 * rows), 1) >> 2)).astype(F32)
-    own_image = jnp.sum(jnp.where(ends_across <= own, 1.0, 0.0), 1, keepdims=True)
-    near_image = jnp.sum(jnp.where(ends_down <= near, 1.0, 0.0), 0, keepdims=True)
+    own = (base + (iota((1, 4 * rows), 1) >> 2)).astype(F32)
+    near = (base - rows + (iota((12 * rows, 1), 0) >> 2)).astype(F32)
+    own_image = jnp.sum(jnp.where(ends_down <= own, 1.0, 0.0), 0, keepdims=True)
+    near_image = jnp.sum(jnp.where(ends_across <= near, 1.0, 0.0), 1, keepdims=True)
     inside = (near >= 0.0) & (near < float(tokens))
     return own_image, jnp.where(inside, near_image, -1.0)
 
@@ -82,6 +82,7 @@
     out_v,
     go,
     wd,
+    wt,
     wu,
     pre,
     qs,
@@ -105,6 +106,8 @@
     back,
     back_in,
     probs,
+    probs_low,
+    ready,
     load_sem,
     down_sem,
     part_s,
@@ -128,8 +131,8 @@
 ):
     sects, groups, spans, near, far, cap, split = sizes
     rows = grad_out.shape[0]
-    hidden = w_up.shape[1]
-    cols = queries.shape[1]
+    hidden = w_up.shape[0]
+    cols = queries.shape[0]
     patches = 4 * rows
     x, g, y = lax.axis_index("sect"), lax.axis_index("grp"), lax.axis_index("span")
     g_hi, g_lo = g // near, g % near
@@ -150,13 +153,17 @@
         return (x, (g + d + groups) % groups, y)
 
     barrier = pltpu.get_barrier_semaphore()
-    peers = [at_far(d) for d in far_first(far)]
+    far_steps = sorted({1 % far, far - 1})
+    peers = [at_far(d) for d in far_steps]
     peers += [at_y(d) for d in range(1, spans)]
     peers += [at_near(d) for d in range(1, near)]
     peers += [at_g(1), at_g(-1)]
     peers += [at_x(d) for d in range(1, sects)]
+    def signal(sem, peer):
+        pl.semaphore_signal(sem, inc=1, device_id=peer, device_id_type=pl.DeviceIdType.MESH)
+
     for peer in peers:
-        pl.semaphore_signal(barrier, inc=1, device_id=peer, device_id_type=pl.DeviceIdType.MESH)
+        signal(barrier, peer)
 
     sent = []
 
@@ -187,22 +194,26 @@
         load_wd.append(load(w_down.at[chunk, :], wd.at[chunk, :], down_sem.at[d]))
     load_len = load(lengths, lens, load_sem.at[2])
     load_q = load(queries, qs, load_sem.at[3])
-    load_k = load(keys, kx.at[pl.ds(patches, patches), :], load_sem.at[4])
-    load_v = load(values, vx.at[pl.ds(patches, patches), :], load_sem.at[5])
+    load_k = load(keys, kx.at[1], load_sem.at[4])
+    load_v = load(values, vx.at[1], load_sem.at[5])
     load_pre = load(pre_act, pre, load_sem.at[6])
-    head_devices = sects * spans
-    for d in range(head_devices):
-        for p in range(4):
-            load(
-                w_up.at[pl.ds((p * head_devices + d) * cols, cols), :],
-                wu.at[pl.ds((d * 4 + p) * cols, cols), :],
-                load_sem.at[7],
-            )
+    load_wt = load(w_up, wt, load_sem.at[7])
 
     load_dst.wait()
     packer, label = token_packing(dst[...], rows, near, far, cap)
+    load_k.wait()
+    load_v.wait()
+    pl.semaphore_wait(barrier, len(peers))
+    for i, d in enumerate(far_steps):
+        signal(ready.at[0, i], at_far(d))
+    halo_copies = []
+    for i, (full, step) in enumerate(((kx, 1), (vx, 1), (kx, -1), (vx, -1))):
+        land = full.at[0 if step == 1 else 2]
+        halo_copies.append(send(full.at[1], land, halo_s.at[i], halo_r.at[i], at_g(step)))
+
     load_go.wait()
     own_part = None
+    part_copies = []
     for d, loaded in zip(order_y, load_wd):
         loaded.wait()
         chunk = pl.ds(pl.multiple_of(((y + d) % spans) * hidden, 16), hidden)
@@ -211,23 +222,17 @@
             own_part = product
         else:
             part[d - 1] = product.astype(BF16)
+            part_copies.append(
+                send(part.at[d - 1], part_in.at[d - 1], part_s.at[d - 1], part_r.at[d - 1], at_y(d))
+            )
     load_len.wait()
     own_image, near_image = image_ids(lens[...], g, rows, rows * groups)
-    load_k.wait()
-    load_v.wait()
-
-    pl.semaphore_wait(barrier, len(peers))
-    part_copies = [
-        send(part.at[d - 1], part_in.at[d - 1], part_s.at[d - 1], part_r.at[d - 1], at_y(d))
-        for d in far_first(spans)
-    ]
-    own_block = pl.ds(patches, patches)
-    halo_copies = []
-    for i, (full, step) in enumerate(((kx, 1), (vx, 1), (kx, -1), (vx, -1))):
-        land = pl.ds(0 if step == 1 else 2 * patches, patches)
-        halo_copies.append(
-            send(full.at[own_block, :], full.at[land, :], halo_s.at[i], halo_r.at[i], at_g(step))
-        )
+    for i in range(len(far_steps)):
+        pl.semaphore_wait(ready.at[0, i], 1)
+    second = [d for d in (1, far - 1, 2, far - 2) if far > 2 and d < far]
+    second = sorted(set(second))
+    for i, d in enumerate(second):
+        signal(ready.at[1, i], at_far(d))
 
     total = own_part
     for d, copy in zip(far_first(spans), part_copies):
@@ -258,6 +263,8 @@
     for copy in near_copies:
         copy.wait_recv()
     far_out[...] = dot(shuffle, near_in[...]).astype(BF16)
+    for i in range(len(second)):
+        pl.semaphore_wait(ready.at[1, i], 1)
     far_copies = []
     for d in far_first(far):
         block = pl.ds(pl.multiple_of(((g_hi + d) % far) * far_rows, far_rows), far_rows)
@@ -274,18 +281,43 @@
     far_in[pl.ds(0, far_rows), :] = far_out[mine, :]
 
     scale = HEAD_DIM ** (-0.5)
+    width = 4 * cols
     load_q.wait()
     for copy in halo_copies:
         copy.wait_recv()
-    scores = dot(qs[...], kx[...], LAST) * scale
-    scores = jnp.where(own_image == near_image, scores, -jnp.inf)
-    top_score = jnp.max(scores, 1, keepdims=True)
-    weights = jnp.exp(scores - top_score)
-    probs[...] = weights / jnp.sum(weights, 1, keepdims=True)
-    attended = dot(probs[...].astype(BF16), vx[...])
+    top_score = None
+    for block in range(3):
+        scores = dot(kx[block], qs[...], FIRST) * scale
+        image = near_image[block * patches : (block + 1) * patches]
+        scores = jnp.where(image == own_image, scores, -jnp.inf)
+        probs[block] = scores
+        top = jnp.max(scores, 0, keepdims=True)
+        top_score = top if top_score is None else jnp.maximum(top_score, top)
+    weight_sum = jnp.zeros((1, patches), F32)
+    for block in range(3):
+        weights = jnp.exp(probs[block] - top_score)
+        probs[block] = weights
+        weight_sum = weight_sum + jnp.sum(weights, 0, keepdims=True)
+    attended = jnp.zeros((cols, patches), F32)
+    for block in range(3):
+        weights = probs[block] / weight_sum
+        probs[block] = weights
+        probs_low[block] = weights.astype(BF16)
+        attended = attended + dot(vx[block], probs_low[block])
     load_pre.wait()
     slope = gelu_slope(pre[...].astype(F32))
-    pltpu.make_async_copy(w_up, wu, load_sem.at[7]).wait()
+    load_wt.wait()
+    step_rows = 32
+
+    def regroup(i, carry):
+        some = pl.ds(pl.multiple_of(i * step_rows, step_rows), step_rows)
+        for d in range(sects * spans):
+            for p in range(4):
+                start = (p * sects * spans + d) * cols
+                wu[d, some, p * cols : (p + 1) * cols] = wt[some, start : start + cols]
+        return carry
+
+    lax.fori_loop(0, hidden // step_rows, regroup, 0)
 
     for copy in far_copies:
         copy.wait_recv()
@@ -295,13 +327,11 @@
     grad_hidden = dot(unpacker.astype(BF16), arrived[:, :hidden], FIRST)
     grad_pre = (grad_hidden * slope).astype(BF16)
     top, low = pl.ds(0, split), pl.ds(split, rows - split)
-    width = 4 * cols
     a_copies, b_copies = {}, {}
     for dx in far_first(sects) + [0]:
         for dy in far_first(spans) + [0]:
             owner = ((x + dx) % sects) * spans + (y + dy) % spans
-            weight = wu[pl.ds(pl.multiple_of(owner * width, 16), width), :]
-            mix[dx, dy] = dot(grad_pre, weight, LAST).astype(BF16)
+            mix[dx, dy] = dot(grad_pre, wu[owner]).astype(BF16)
             if dx:
                 a_copies[dx, dy] = send(
                     mix.at[dx, dy, top, :],
@@ -352,25 +382,22 @@
         share_b = share_b + fin_b[d].astype(F32)
     share = jnp.concatenate([share_a, share_b], 0).astype(BF16)
 
-    patch_row, token = iota((patches, rows), 0), iota((patches, rows), 1)
-    grad_attn = jnp.zeros((patches, cols), F32)
+    token, patch = iota((rows, patches), 0), iota((rows, patches), 1)
+    grad_attn = jnp.zeros((cols, patches), F32)
     for p in range(4):
-        spread = jnp.where(patch_row == 4 * token + p, 1.0, 0.0).astype(BF16)
-        grad_attn = grad_attn + dot(spread, share[:, p * cols : (p + 1) * cols])
-    row_delta = jnp.sum(grad_attn.astype(BF16).astype(F32) * attended, 1, keepdims=True)
+        spread = jnp.where(patch == 4 * token + p, 1.0, 0.0).astype(BF16)
+        grad_attn = grad_attn + dot(share[:, p * cols : (p + 1) * cols], spread, FIRST)
+    row_delta = jnp.sum(grad_attn * attended, 0, keepdims=True)
     grad_attn = grad_attn.astype(BF16)
-    grad_scores = []
     back_copies = []
     q = qs[...]
     kept = None
+    grad_query = jnp.zeros((cols, patches), F32)
     for block in (0, 2, 1):
-        lanes = pl.ds(block * patches, patches)
-        weights = probs[:, lanes]
-        grad_probs = dot(grad_attn, vx[lanes, :], LAST)
-        score_part = (weights * (grad_probs - row_delta)).astype(BF16)
-        value_part = dot(weights.astype(BF16), grad_attn, FIRST)
-        key_part = dot(score_part, q, FIRST) * scale
-        grad_scores.append((lanes, score_part))
+        grad_probs = dot(vx[block], grad_attn, FIRST)
+        score_part = (probs[block] * (grad_probs - row_delta)).astype(BF16)
+        value_part = dot(grad_attn, probs_low[block], LAST)
+        key_part = dot(q, score_part, LAST) * scale
         if block == 1:
             kept = key_part, value_part
         else:
@@ -386,9 +413,7 @@
                     at_g(block - 1),
                 )
             )
-    grad_query = jnp.zeros((patches, cols), F32)
-    for lanes, score_part in grad_scores:
-        grad_query = grad_query + dot(score_part, kx[lanes, :])
+        grad_query = grad_query + dot(kx[block], score_part)
     out_q[...] = (grad_query * scale).astype(BF16)
     key_part, value_part = kept
     for copy in back_copies:
@@ -420,9 +445,9 @@
     dma = pltpu.SemaphoreType.DMA
     vmem = pltpu.VMEM
     some = pl.BlockSpec(memory_space=pl.ANY)
-    out = jax.ShapeDtypeStruct((patches, cols), BF16)
+    out = jax.ShapeDtypeStruct((cols, patches), BF16)
     sizes = (sects, groups, spans, near, far, cap, split)
-    return pl.pallas_call(
+    outs = pl.pallas_call(
         functools.partial(kernel, sizes),
         out_shape=(out, out, out),
         in_specs=[some] * 9,
@@ -430,11 +455,12 @@
         scratch_shapes=[
             vmem((rows, merged), BF16),
             vmem(w_down.shape, BF16),
-            vmem((merge_rows, hidden), BF16),
+            vmem((hidden, merge_rows), BF16),
+            vmem((sects * spans, hidden, width), BF16),
             vmem((rows, hidden), BF16),
-            vmem((patches, cols), BF16),
-            vmem((3 * patches, cols), BF16),
-            vmem((3 * patches, cols), BF16),
+            vmem((cols, patches), BF16),
+            vmem((3, cols, patches), BF16),
+            vmem((3, cols, patches), BF16),
             vmem((1, rows), jnp.int32),
             vmem((1, lengths.shape[0]), jnp.int32),
             vmem((spans - 1, rows, hidden), BF16),
@@ -450,9 +476,11 @@
             vmem((sects - 1, rows - split, width), BF16),
             vmem((spans - 1, split, width), BF16),
             vmem((sects - 1, rows - split, width), BF16),
-            vmem((2, 2, patches, cols), BF16),
-            vmem((2, 2, patches, cols), BF16),
-            vmem((patches, 3 * patches), F32),
+            vmem((2, 2, cols, patches), BF16),
+            vmem((2, 2, cols, patches), BF16),
+            vmem((3, patches, patches), F32),
+            vmem((3, patches, patches), BF16),
+            pltpu.SemaphoreType.REGULAR((2, 4)),
             dma((8,)),
             dma((spans,)),
             dma((spans - 1,)),
@@ -483,12 +511,13 @@
         destination.reshape(1, rows),
         w_down,
         pre_act,
-        w_up,
-        queries,
-        key_states,
-        value_states,
+        w_up.T,
+        queries.T,
+        key_states.T,
+        value_states.T,
         lengths.reshape(1, lengths.shape[0]),
     )
+    return tuple(each.T for each in outs)
 
 
 def solution(mesh):

time: 88.6 us -> 70.8 us (0.80)
  local copies, waits for them, and re-layouts: 15.3 us -> 4.38 us
  Pallas kernels: 72.1 us -> 65.4 us
    pallas_call x1, Pallas kernels: 72.1 us -> 65.4 us  [on_device(): pl.pallas_call(functools.partial(kernel, sizes), out_shape=(out, out, out...]
    unnamed x4 -> x3, local copies, waits for them, and re-layouts: 10.5 us -> 4.38 us
    pallas_call x3 -> x0, local copies, waits for them, and re-layouts: 4.81 us -> none  [on_device(): pl.pallas_call(functools.partial(kernel, sizes), out_shape=(out, out, out...]
where the time goes in v3:
time: 70.8 us; the launch traced here: 70.5 us
  Pallas kernels  65.4 us (92%)
  local copies, waits for them, and re-layouts  4.38 us (6%)
    pallas_call x1, Pallas kernels, on_device(): pl.pallas_call(functools.partial(kernel, sizes), out_shape=(out, out, out...  65.4 us
    unnamed x3, local copies, waits for them, and re-layouts  4.38 us

profile of v3, /device:TPU:1, one launch (start us, length us, event | category | flops | bytes accessed | tf_op | source)
XLA Modules:
  0.0 70.5 jit_solution(1573888578251952243)
XLA Ops:
  0.6 65.4 %merger_attention_backward.1 = (bf16[80,320]{1,0:T(8,128)(2,1)}, bf16[80,320]{1,0:T(8,128)(2,1)}, bf16[80,320]{1,0:T(8,128)(2,1)}) custom-call(bf16[80,2048]{1,0:T(8,128)(2,1)} %grad_out.1, s32[1,80]{1,0:T(1,128)} %bitcast.17, bf16[1280,2048]{1,0:T(8,128)(2,1)} %w_down.1, bf16[80,320]{1,0:T(8,128)(2,1)} %pre_act.1, bf16[320,5120]{1,0:T(8,128)(2,1)} %bitcast.9, ...), custom_call_target="tpu_custom_call" | custom-call | tf_op jit(solution)/shard_map/merger_attention_backward/pallas_call | solution.py:450
  66.1 1.5 %copy.15 = bf16[320,80]{0,1:T(8,128)(2,1)} copy(bf16[320,80]{0,1:T(8,128)(2,1)} %bitcast.15) | data formatting | bytes 102400
  67.5 1.5 %copy.16 = bf16[320,80]{0,1:T(8,128)(2,1)} copy(bf16[320,80]{0,1:T(8,128)(2,1)} %bitcast.14) | data formatting | bytes 102400
  69.0 1.5 %copy.17 = bf16[320,80]{0,1:T(8,128)(2,1)} copy(bf16[320,80]{0,1:T(8,128)(2,1)} %bitcast.13) | data formatting | bytes 102400

commit v4 on v3

--- a/solution.py
+++ b/solution.py
@@ -26,6 +26,10 @@
 def gelu_slope(values):
     normal_cdf = 0.5 * (1.0 + lax.erf(values * 0.7071067811865476))
     return normal_cdf + values * jnp.exp(-0.5 * values * values) * 0.3989422804014327
+
+
+def log2(n):
+    return n.bit_length() - 1
 
 
 def far_first(n):
@@ -107,6 +111,11 @@
     back_in,
     probs,
     probs_low,
+    pack,
+    swap,
+    spread,
+    slopes,
+    own_part,
     ready,
     load_sem,
     down_sem,
@@ -152,19 +161,6 @@
     def at_g(d):
         return (x, (g + d + groups) % groups, y)
 
-    barrier = pltpu.get_barrier_semaphore()
-    far_steps = sorted({1 % far, far - 1})
-    peers = [at_far(d) for d in far_steps]
-    peers += [at_y(d) for d in range(1, spans)]
-    peers += [at_near(d) for d in range(1, near)]
-    peers += [at_g(1), at_g(-1)]
-    peers += [at_x(d) for d in range(1, sects)]
-    def signal(sem, peer):
-        pl.semaphore_signal(sem, inc=1, device_id=peer, device_id_type=pl.DeviceIdType.MESH)
-
-    for peer in peers:
-        signal(barrier, peer)
-
     sent = []
 
     def send(src, to, send_sem, recv_sem, peer):
@@ -189,44 +185,62 @@
     load_go = load(grad_out, go, load_sem.at[0])
     load_dst = load(dest, dst, load_sem.at[1])
     load_wd = []
+    load_k = load(keys, kx.at[1], load_sem.at[4])
+    load_v = load(values, vx.at[1], load_sem.at[5])
     for d in order_y:
         chunk = pl.ds(pl.multiple_of(((y + d) % spans) * hidden, 16), hidden)
         load_wd.append(load(w_down.at[chunk, :], wd.at[chunk, :], down_sem.at[d]))
     load_len = load(lengths, lens, load_sem.at[2])
     load_q = load(queries, qs, load_sem.at[3])
-    load_k = load(keys, kx.at[1], load_sem.at[4])
-    load_v = load(values, vx.at[1], load_sem.at[5])
     load_pre = load(pre_act, pre, load_sem.at[6])
     load_wt = load(w_up, wt, load_sem.at[7])
 
-    load_dst.wait()
-    packer, label = token_packing(dst[...], rows, near, far, cap)
-    load_k.wait()
-    load_v.wait()
-    pl.semaphore_wait(barrier, len(peers))
-    for i, d in enumerate(far_steps):
-        signal(ready.at[0, i], at_far(d))
-    halo_copies = []
-    for i, (full, step) in enumerate(((kx, 1), (vx, 1), (kx, -1), (vx, -1))):
-        land = full.at[0 if step == 1 else 2]
-        halo_copies.append(send(full.at[1], land, halo_s.at[i], halo_r.at[i], at_g(step)))
+    barrier = pltpu.get_barrier_semaphore()
+    far_steps = sorted({1 % far, far - 1})
+    peers = [at_far(d) for d in far_steps]
+    peers += [at_y(d) for d in range(1, spans)]
+    peers += [at_near(d) for d in range(1, near)]
+    peers += [at_g(1), at_g(-1)]
+    peers += [at_x(d) for d in range(1, sects)]
+    def signal(sem, peer):
+        pl.semaphore_signal(sem, inc=1, device_id=peer, device_id_type=pl.DeviceIdType.MESH)
+
+    for peer in peers:
+        signal(barrier, peer)
 
     load_go.wait()
-    own_part = None
     part_copies = []
     for d, loaded in zip(order_y, load_wd):
         loaded.wait()
         chunk = pl.ds(pl.multiple_of(((y + d) % spans) * hidden, 16), hidden)
         product = dot(go[...], wd[chunk, :], LAST)
         if d == 0:
-            own_part = product
-        else:
-            part[d - 1] = product.astype(BF16)
-            part_copies.append(
-                send(part.at[d - 1], part_in.at[d - 1], part_s.at[d - 1], part_r.at[d - 1], at_y(d))
-            )
-    load_len.wait()
-    own_image, near_image = image_ids(lens[...], g, rows, rows * groups)
+            own_part[...] = product
+            continue
+        part[d - 1] = product.astype(BF16)
+        if not part_copies:
+            pl.semaphore_wait(barrier, len(peers))
+            for i, step in enumerate(far_steps):
+                signal(ready.at[0, i], at_far(step))
+        part_copies.append(
+            send(part.at[d - 1], part_in.at[d - 1], part_s.at[d - 1], part_r.at[d - 1], at_y(d))
+        )
+    load_k.wait()
+    load_v.wait()
+    halo_copies = []
+    for i, (full, step) in enumerate(((kx, 1), (vx, 1), (kx, -1), (vx, -1))):
+        land = full.at[0 if step == 1 else 2]
+        halo_copies.append(send(full.at[1], land, halo_s.at[i], halo_r.at[i], at_g(step)))
+    load_dst.wait()
+    pack[...], label = token_packing(dst[...], rows, near, far, cap)
+    near_out[:, hidden:] = jnp.broadcast_to(label, (near * far * cap, LABEL_LANES)).astype(BF16)
+    slots = near * far * cap
+    near_rows, far_rows = far * cap, near * cap
+    out_row = iota((slots, slots), 0)
+    in_row = iota((slots, slots), 1)
+    source = ((out_row >> log2(cap)) & (near - 1)) * near_rows
+    source = source + (out_row >> log2(far_rows)) * cap + (out_row & (cap - 1))
+    swap[...] = jnp.where(source == in_row, 1.0, 0.0).astype(BF16)
     for i in range(len(far_steps)):
         pl.semaphore_wait(ready.at[0, i], 1)
     second = [d for d in (1, far - 1, 2, far - 2) if far > 2 and d < far]
@@ -234,14 +248,11 @@
     for i, d in enumerate(second):
         signal(ready.at[1, i], at_far(d))
 
-    total = own_part
+    total = own_part[...]
     for d, copy in zip(far_first(spans), part_copies):
         copy.wait_recv()
         total = total + part_in[d - 1].astype(F32)
-    slots = near * far * cap
-    near_rows, far_rows = far * cap, near * cap
-    near_out[:, :hidden] = dot(packer, total.astype(BF16)).astype(BF16)
-    near_out[:, hidden:] = jnp.broadcast_to(label, (slots, LABEL_LANES)).astype(BF16)
+    near_out[:, :hidden] = dot(pack[...], total.astype(BF16)).astype(BF16)
     near_copies = []
     for d in range(near - 1, 0, -1):
         block = pl.ds(pl.multiple_of(((g_lo + d) % near) * near_rows, near_rows), near_rows)
@@ -256,17 +267,14 @@
         )
     mine = pl.ds(pl.multiple_of(g_lo * near_rows, near_rows), near_rows)
     near_in[pl.ds(0, near_rows), :] = near_out[mine, :]
-    out_row = iota((slots, slots), 0)
-    in_row = iota((slots, slots), 1)
-    source = ((out_row // cap) % near) * near_rows + (out_row // far_rows) * cap + out_row % cap
-    shuffle = jnp.where(source == in_row, 1.0, 0.0).astype(BF16)
     for copy in near_copies:
         copy.wait_recv()
-    far_out[...] = dot(shuffle, near_in[...]).astype(BF16)
+    far_out[...] = dot(swap[...], near_in[...]).astype(BF16)
     for i in range(len(second)):
         pl.semaphore_wait(ready.at[1, i], 1)
     far_copies = []
-    for d in far_first(far):
+
+    def release(d):
         block = pl.ds(pl.multiple_of(((g_hi + d) % far) * far_rows, far_rows), far_rows)
         far_copies.append(
             send(
@@ -277,6 +285,10 @@
                 at_far(d),
             )
         )
+    waves = [[d for d in far_first(far) if min(d, far - d) == k] for k in range(far // 2, 0, -1)]
+    waves += [[]] * (4 - len(waves))
+    for d in waves[0] + waves[1]:
+        release(d)
     mine = pl.ds(pl.multiple_of(g_hi * far_rows, far_rows), far_rows)
     far_in[pl.ds(0, far_rows), :] = far_out[mine, :]
 
@@ -285,6 +297,8 @@
     load_q.wait()
     for copy in halo_copies:
         copy.wait_recv()
+    load_len.wait()
+    own_image, near_image = image_ids(lens[...], g, rows, rows * groups)
     top_score = None
     for block in range(3):
         scores = dot(kx[block], qs[...], FIRST) * scale
@@ -304,8 +318,13 @@
         probs[block] = weights
         probs_low[block] = weights.astype(BF16)
         attended = attended + dot(vx[block], probs_low[block])
+    for d in waves[2]:
+        release(d)
     load_pre.wait()
-    slope = gelu_slope(pre[...].astype(F32))
+    slopes[...] = gelu_slope(pre[...].astype(F32))
+    token, patch = iota((rows, patches), 0), iota((rows, patches), 1)
+    for p in range(4):
+        spread[p] = jnp.where(patch == 4 * token + p, 1.0, 0.0).astype(BF16)
     load_wt.wait()
     step_rows = 32
 
@@ -319,13 +338,16 @@
 
     lax.fori_loop(0, hidden // step_rows, regroup, 0)
 
+    for d in waves[3]:
+        release(d)
+
     for copy in far_copies:
         copy.wait_recv()
     arrived = far_in[...]
     place = arrived[:, hidden : hidden + 1].astype(F32)
     unpacker = jnp.where(place == (iota((slots, rows), 1) + 1).astype(F32), 1.0, 0.0)
     grad_hidden = dot(unpacker.astype(BF16), arrived[:, :hidden], FIRST)
-    grad_pre = (grad_hidden * slope).astype(BF16)
+    grad_pre = (grad_hidden * slopes[...]).astype(BF16)
     top, low = pl.ds(0, split), pl.ds(split, rows - split)
     a_copies, b_copies = {}, {}
     for dx in far_first(sects) + [0]:
@@ -349,31 +371,32 @@
                     at_y(dy),
                 )
     a2_copies, b2_copies = [], []
-    share_a = share_b = None
-    for dy in far_first(spans) + [0]:
+
+    def sum_top(dy):
         total = mix[0, dy, top, :].astype(F32)
         for dx in far_first(sects):
             a_copies[dx, dy].wait_recv()
             total = total + mix_a[dx - 1, dy].astype(F32)
-        if dy:
-            sum_a[dy - 1] = total.astype(BF16)
-            a2_copies.append(
-                send(sum_a.at[dy - 1], fin_a.at[dy - 1], a2_s.at[dy - 1], a2_r.at[dy - 1], at_y(dy))
-            )
-        else:
-            share_a = total
-    for dx in far_first(sects) + [0]:
+        return total
+
+    def sum_low(dx):
         total = mix[dx, 0, low, :].astype(F32)
         for dy in far_first(spans):
             b_copies[dx, dy].wait_recv()
             total = total + mix_b[dy - 1, dx].astype(F32)
-        if dx:
-            sum_b[dx - 1] = total.astype(BF16)
-            b2_copies.append(
-                send(sum_b.at[dx - 1], fin_b.at[dx - 1], b2_s.at[dx - 1], b2_r.at[dx - 1], at_x(dx))
-            )
-        else:
-            share_b = total
+        return total
+
+    for d in far_first(sects):
+        sum_b[d - 1] = sum_low(d).astype(BF16)
+        b2_copies.append(
+            send(sum_b.at[d - 1], fin_b.at[d - 1], b2_s.at[d - 1], b2_r.at[d - 1], at_x(d))
+        )
+    for d in far_first(spans):
+        sum_a[d - 1] = sum_top(d).astype(BF16)
+        a2_copies.append(
+            send(sum_a.at[d - 1], fin_a.at[d - 1], a2_s.at[d - 1], a2_r.at[d - 1], at_y(d))
+        )
+    share_b, share_a = sum_low(0), sum_top(0)
     for copy in a2_copies + b2_copies:
         copy.wait_recv()
     for d in range(spans - 1):
@@ -382,11 +405,9 @@
         share_b = share_b + fin_b[d].astype(F32)
     share = jnp.concatenate([share_a, share_b], 0).astype(BF16)
 
-    token, patch = iota((rows, patches), 0), iota((rows, patches), 1)
     grad_attn = jnp.zeros((cols, patches), F32)
     for p in range(4):
-        spread = jnp.where(patch == 4 * token + p, 1.0, 0.0).astype(BF16)
-        grad_attn = grad_attn + dot(share[:, p * cols : (p + 1) * cols], spread, FIRST)
+        grad_attn = grad_attn + dot(share[:, p * cols : (p + 1) * cols], spread[p], FIRST)
     row_delta = jnp.sum(grad_attn * attended, 0, keepdims=True)
     grad_attn = grad_attn.astype(BF16)
     back_copies = []
@@ -425,6 +446,12 @@
     out_v[...] = value_part.astype(BF16)
     for copy in sent:
         copy.wait_send()
+
+
+def move(*refs):
+    half = len(refs) // 2
+    for source, target in zip(refs[:half], refs[half:]):
+        target[...] = source[...]
 
 
 def on_device(
@@ -480,6 +507,11 @@
             vmem((2, 2, cols, patches), BF16),
             vmem((3, patches, patches), F32),
             vmem((3, patches, patches), BF16),
+            vmem((slots, rows), BF16),
+            vmem((slots, slots), BF16),
+            vmem((4, rows, patches), BF16),
+            vmem((rows, hidden), F32),
+            vmem((rows, hidden), F32),
             pltpu.SemaphoreType.REGULAR((2, 4)),
             dma((8,)),
             dma((spans,)),
@@ -517,6 +549,13 @@
         value_states.T,
         lengths.reshape(1, lengths.shape[0]),
     )
+    outs = pl.pallas_call(
+        move,
+        out_shape=(out, out, out),
+        in_specs=[pl.BlockSpec(memory_space=pltpu.VMEM)] * 3,
+        out_specs=[pl.BlockSpec(memory_space=pltpu.VMEM)] * 3,
+        name="gradients_out",
+    )(*outs)
     return tuple(each.T for each in outs)
 
 

time: 70.8 us -> 65.5 us (0.925)
  local copies, waits for them, and re-layouts: 4.38 us -> 0 us
  Pallas kernels: 65.4 us -> 64.6 us
    unnamed x3 -> x0, local copies, waits for them, and re-layouts: 4.38 us -> none
    pallas_call x1, Pallas kernels: 65.4 us -> 63.1 us  [on_device(): pl.pallas_call(functools.partial(kernel, sizes), out_shape=(out, out, out...]
    pallas_call x0 -> x1, Pallas kernels: none -> 1.56 us  [on_device(): pl.pallas_call(move, out_shape=(out, out, out), in_specs=[pl.BlockSpec(me...]
where the time goes in v4:
time: 65.5 us; the launch traced here: 65.3 us
  Pallas kernels  64.6 us (99%)
    pallas_call x1, Pallas kernels, on_device(): pl.pallas_call(functools.partial(kernel, sizes), out_shape=(out, out, out...  63.1 us
    pallas_call x1, Pallas kernels, on_device(): pl.pallas_call(move, out_shape=(out, out, out), in_specs=[pl.BlockSpec(me...  1.56 us

profile of v4, /device:TPU:1, one launch (start us, length us, event | category | flops | bytes accessed | tf_op | source)
XLA Modules:
  0.0 65.3 jit_solution(12944418882296949182)
XLA Ops:
  0.6 63.1 %merger_attention_backward.1 = (bf16[80,320]{1,0:T(8,128)(2,1)}, bf16[80,320]{1,0:T(8,128)(2,1)}, bf16[80,320]{1,0:T(8,128)(2,1)}) custom-call(bf16[80,2048]{1,0:T(8,128)(2,1)} %grad_out.1, s32[1,80]{1,0:T(1,128)} %bitcast.14, bf16[1280,2048]{1,0:T(8,128)(2,1)} %w_down.1, bf16[80,320]{1,0:T(8,128)(2,1)} %pre_act.1, bf16[320,5120]{1,0:T(8,128)(2,1)} %bitcast.9, ...), custom_call_target="tpu_custom_call" | custom-call | tf_op jit(solution)/shard_map/merger_attention_backward/pallas_call | solution.py:477
  63.7 1.6 %gradients_out.1 = (bf16[80,320]{1,0:T(8,128)(2,1)}, bf16[80,320]{1,0:T(8,128)(2,1)}, bf16[80,320]{1,0:T(8,128)(2,1)}) custom-call(bf16[80,320]{1,0:T(8,128)(2,1)} %get-tuple-element.9.refs_0_, bf16[80,320]{1,0:T(8,128)(2,1)} %get-tuple-element.10.refs_1_, bf16[80,320]{1,0:T(8,128)(2,1)} %get-tuple-element.11.refs_2_), custom_call_target="tpu_custom_call" | custom-call | tf_op jit(solution)/shard_map/gradients_out/pallas_call | solution.py:552

commit v5 on v4

--- a/solution.py
+++ b/solution.py
@@ -101,12 +101,7 @@
     far_out,
     far_in,
     mix,
-    mix_a,
-    mix_b,
-    fin_a,
-    fin_b,
-    sum_a,
-    sum_b,
+    mix_in,
     back,
     back_in,
     probs,
@@ -127,18 +122,12 @@
     near_r,
     far_s,
     far_r,
-    a1_s,
-    a1_r,
-    b1_s,
-    b1_r,
-    a2_s,
-    a2_r,
-    b2_s,
-    b2_r,
+    mix_s,
+    mix_r,
     back_s,
     back_r,
 ):
-    sects, groups, spans, near, far, cap, split = sizes
+    sects, groups, spans, near, far, cap = sizes
     rows = grad_out.shape[0]
     hidden = w_up.shape[0]
     cols = queries.shape[0]
@@ -146,8 +135,14 @@
     x, g, y = lax.axis_index("sect"), lax.axis_index("grp"), lax.axis_index("span")
     g_hi, g_lo = g // near, g % near
 
-    def at_x(d):
-        return ((x + d) % sects, g, y)
+    def at_xy(dx, dy):
+        return ((x + dx) % sects, g, (y + dy) % spans)
+
+    def hops(pair):
+        return min(pair[0], sects - pair[0]) + min(pair[1], spans - pair[1])
+
+    others = [(dx, dy) for dx in range(sects) for dy in range(spans) if dx or dy]
+    others.sort(key=hops, reverse=True)
 
     def at_y(d):
         return (x, g, (y + d) % spans)
@@ -198,10 +193,9 @@
     barrier = pltpu.get_barrier_semaphore()
     far_steps = sorted({1 % far, far - 1})
     peers = [at_far(d) for d in far_steps]
-    peers += [at_y(d) for d in range(1, spans)]
     peers += [at_near(d) for d in range(1, near)]
     peers += [at_g(1), at_g(-1)]
-    peers += [at_x(d) for d in range(1, sects)]
+    peers += [at_xy(dx, dy) for dx, dy in others]
     def signal(sem, peer):
         pl.semaphore_signal(sem, inc=1, device_id=peer, device_id_type=pl.DeviceIdType.MESH)
 
@@ -318,8 +312,6 @@
         probs[block] = weights
         probs_low[block] = weights.astype(BF16)
         attended = attended + dot(vx[block], probs_low[block])
-    for d in waves[2]:
-        release(d)
     load_pre.wait()
     slopes[...] = gelu_slope(pre[...].astype(F32))
     token, patch = iota((rows, patches), 0), iota((rows, patches), 1)
@@ -336,7 +328,11 @@
                 wu[d, some, p * cols : (p + 1) * cols] = wt[some, start : start + cols]
         return carry
 
-    lax.fori_loop(0, hidden // step_rows, regroup, 0)
+    halves = hidden // step_rows // 2
+    lax.fori_loop(0, halves, regroup, 0)
+    for d in waves[2]:
+        release(d)
+    lax.fori_loop(halves, hidden // step_rows, regroup, 0)
 
     for d in waves[3]:
         release(d)
@@ -348,63 +344,19 @@
     unpacker = jnp.where(place == (iota((slots, rows), 1) + 1).astype(F32), 1.0, 0.0)
     grad_hidden = dot(unpacker.astype(BF16), arrived[:, :hidden], FIRST)
     grad_pre = (grad_hidden * slopes[...]).astype(BF16)
-    top, low = pl.ds(0, split), pl.ds(split, rows - split)
-    a_copies, b_copies = {}, {}
-    for dx in far_first(sects) + [0]:
-        for dy in far_first(spans) + [0]:
-            owner = ((x + dx) % sects) * spans + (y + dy) % spans
-            mix[dx, dy] = dot(grad_pre, wu[owner]).astype(BF16)
-            if dx:
-                a_copies[dx, dy] = send(
-                    mix.at[dx, dy, top, :],
-                    mix_a.at[dx - 1, dy],
-                    a1_s.at[dx - 1, dy],
-                    a1_r.at[dx - 1, dy],
-                    at_x(dx),
-                )
-            if dy:
-                b_copies[dx, dy] = send(
-                    mix.at[dx, dy, low, :],
-                    mix_b.at[dy - 1, dx],
-                    b1_s.at[dy - 1, dx],
-                    b1_r.at[dy - 1, dx],
-                    at_y(dy),
-                )
-    a2_copies, b2_copies = [], []
-
-    def sum_top(dy):
-        total = mix[0, dy, top, :].astype(F32)
-        for dx in far_first(sects):
-            a_copies[dx, dy].wait_recv()
-            total = total + mix_a[dx - 1, dy].astype(F32)
-        return total
-
-    def sum_low(dx):
-        total = mix[dx, 0, low, :].astype(F32)
-        for dy in far_first(spans):
-            b_copies[dx, dy].wait_recv()
-            total = total + mix_b[dy - 1, dx].astype(F32)
-        return total
-
-    for d in far_first(sects):
-        sum_b[d - 1] = sum_low(d).astype(BF16)
-        b2_copies.append(
-            send(sum_b.at[d - 1], fin_b.at[d - 1], b2_s.at[d - 1], b2_r.at[d - 1], at_x(d))
+    mix_copies = []
+    for dx, dy in others:
+        owner = ((x + dx) % sects) * spans + (y + dy) % spans
+        i = dx * spans + dy - 1
+        mix[i] = dot(grad_pre, wu[owner]).astype(BF16)
+        mix_copies.append(
+            (i, send(mix.at[i], mix_in.at[i], mix_s.at[i], mix_r.at[i], at_xy(dx, dy)))
         )
-    for d in far_first(spans):
-        sum_a[d - 1] = sum_top(d).astype(BF16)
-        a2_copies.append(
-            send(sum_a.at[d - 1], fin_a.at[d - 1], a2_s.at[d - 1], a2_r.at[d - 1], at_y(d))
-        )
-    share_b, share_a = sum_low(0), sum_top(0)
-    for copy in a2_copies + b2_copies:
+    share = dot(grad_pre, wu[x * spans + y])
+    for i, copy in mix_copies:
         copy.wait_recv()
-    for d in range(spans - 1):
-        share_a = share_a + fin_a[d].astype(F32)
-    for d in range(sects - 1):
-        share_b = share_b + fin_b[d].astype(F32)
-    share = jnp.concatenate([share_a, share_b], 0).astype(BF16)
-
+        share = share + mix_in[i].astype(F32)
+    share = share.astype(BF16)
     grad_attn = jnp.zeros((cols, patches), F32)
     for p in range(4):
         grad_attn = grad_attn + dot(share[:, p * cols : (p + 1) * cols], spread[p], FIRST)
@@ -412,31 +364,39 @@
     grad_attn = grad_attn.astype(BF16)
     back_copies = []
     q = qs[...]
-    kept = None
+
+    def give_back(block, kind, term):
+        side = block // 2
+        back[side, kind] = term.astype(BF16)
+        back_copies.append(
+            send(
+                back.at[side, kind],
+                back_in.at[1 - side, kind],
+                back_s.at[side, kind],
+                back_r.at[1 - side, kind],
+                at_g(block - 1),
+            )
+        )
+
+    def value_term(block):
+        return dot(grad_attn, probs_low[block], LAST)
+
+    def score_term(block):
+        grad_probs = dot(vx[block], grad_attn, FIRST)
+        return (probs[block] * (grad_probs - row_delta)).astype(BF16)
+
+    for block in (0, 2):
+        give_back(block, 1, value_term(block))
     grad_query = jnp.zeros((cols, patches), F32)
-    for block in (0, 2, 1):
-        grad_probs = dot(vx[block], grad_attn, FIRST)
-        score_part = (probs[block] * (grad_probs - row_delta)).astype(BF16)
-        value_part = dot(grad_attn, probs_low[block], LAST)
-        key_part = dot(q, score_part, LAST) * scale
-        if block == 1:
-            kept = key_part, value_part
-        else:
-            side = block // 2
-            back[side, 0] = key_part.astype(BF16)
-            back[side, 1] = value_part.astype(BF16)
-            back_copies.append(
-                send(
-                    back.at[side],
-                    back_in.at[1 - side],
-                    back_s.at[side],
-                    back_r.at[1 - side],
-                    at_g(block - 1),
-                )
-            )
+    for block in (0, 2):
+        score_part = score_term(block)
+        give_back(block, 0, dot(q, score_part, LAST) * scale)
         grad_query = grad_query + dot(kx[block], score_part)
+    score_part = score_term(1)
+    key_part = dot(q, score_part, LAST) * scale
+    value_part = value_term(1)
+    grad_query = grad_query + dot(kx[1], score_part)
     out_q[...] = (grad_query * scale).astype(BF16)
-    key_part, value_part = kept
     for copy in back_copies:
         copy.wait_recv()
     for side in range(2):
@@ -466,14 +426,13 @@
     far = groups // near
     cap = rows // min(groups, rows // 2)
     slots = groups * cap
-    split = (rows * 5 // 8 // 16) * 16 if rows >= 32 else rows // 2
     width = 4 * cols
     wide = hidden + LABEL_LANES
     dma = pltpu.SemaphoreType.DMA
     vmem = pltpu.VMEM
     some = pl.BlockSpec(memory_space=pl.ANY)
     out = jax.ShapeDtypeStruct((cols, patches), BF16)
-    sizes = (sects, groups, spans, near, far, cap, split)
+    sizes = (sects, groups, spans, near, far, cap)
     outs = pl.pallas_call(
         functools.partial(kernel, sizes),
         out_shape=(out, out, out),
@@ -496,13 +455,8 @@
             vmem((slots, wide), BF16),
             vmem((slots, wide), BF16),
             vmem((slots, wide), BF16),
-            vmem((sects, spans, rows, width), BF16),
-            vmem((sects - 1, spans, split, width), BF16),
-            vmem((spans - 1, sects, rows - split, width), BF16),
-            vmem((spans - 1, split, width), BF16),
-            vmem((sects - 1, rows - split, width), BF16),
-            vmem((spans - 1, split, width), BF16),
-            vmem((sects - 1, rows - split, width), BF16),
+            vmem((sects * spans - 1, rows, width), BF16),
+            vmem((sects * spans - 1, rows, width), BF16),
             vmem((2, 2, cols, patches), BF16),
             vmem((2, 2, cols, patches), BF16),
             vmem((3, patches, patches), F32),
@@ -523,16 +477,10 @@
             dma((near - 1,)),
             dma((far - 1,)),
             dma((far - 1,)),
-            dma((sects - 1, spans)),
-            dma((sects - 1, spans)),
-            dma((spans - 1, sects)),
-            dma((spans - 1, sects)),
-            dma((spans - 1,)),
-            dma((spans - 1,)),
-            dma((sects - 1,)),
-            dma((sects - 1,)),
-            dma((2,)),
-            dma((2,)),
+            dma((sects * spans - 1,)),
+            dma((sects * spans - 1,)),
+            dma((2, 2)),
+            dma((2, 2)),
         ],
         compiler_params=pltpu.CompilerParams(
             collective_id=0, has_side_effects=True, vmem_limit_bytes=60 * 1024 * 1024

time: 65.5 us -> 67.2 us (1.026)
  Pallas kernels: 64.6 us -> 66.4 us
    pallas_call x1, Pallas kernels: 63.1 us -> 64.8 us  [on_device(): pl.pallas_call(functools.partial(kernel, sizes), out_shape=(out, out, out...]
where the time goes in v5:
time: 67.2 us; the launch traced here: 67 us
  Pallas kernels  66.4 us (99%)
    pallas_call x1, Pallas kernels, on_device(): pl.pallas_call(functools.partial(kernel, sizes), out_shape=(out, out, out...  64.8 us
    pallas_call x1, Pallas kernels, on_device(): pl.pallas_call(move, out_shape=(out, out, out), in_specs=[pl.BlockSpec(me...  1.56 us

profile of v5, /device:TPU:1, one launch (start us, length us, event | category | flops | bytes accessed | tf_op | source)
XLA Modules:
  0.0 67.0 jit_solution(6603053297019918958)
XLA Ops:
  0.6 64.8 %merger_attention_backward.1 = (bf16[80,320]{1,0:T(8,128)(2,1)}, bf16[80,320]{1,0:T(8,128)(2,1)}, bf16[80,320]{1,0:T(8,128)(2,1)}) custom-call(bf16[80,2048]{1,0:T(8,128)(2,1)} %grad_out.1, s32[1,80]{1,0:T(1,128)} %bitcast.14, bf16[1280,2048]{1,0:T(8,128)(2,1)} %w_down.1, bf16[80,320]{1,0:T(8,128)(2,1)} %pre_act.1, bf16[320,5120]{1,0:T(8,128)(2,1)} %bitcast.9, ...), custom_call_target="tpu_custom_call" | custom-call | tf_op jit(solution)/shard_map/merger_attention_backward/pallas_call | solution.py:436
  65.5 1.6 %gradients_out.1 = (bf16[80,320]{1,0:T(8,128)(2,1)}, bf16[80,320]{1,0:T(8,128)(2,1)}, bf16[80,320]{1,0:T(8,128)(2,1)}) custom-call(bf16[80,320]{1,0:T(8,128)(2,1)} %get-tuple-element.9.refs_0_, bf16[80,320]{1,0:T(8,128)(2,1)} %get-tuple-element.10.refs_1_, bf16[80,320]{1,0:T(8,128)(2,1)} %get-tuple-element.11.refs_2_), custom_call_target="tpu_custom_call" | custom-call | tf_op jit(solution)/shard_map/gradients_out/pallas_call | solution.py:500

commit v6 on v5

--- a/solution.py
+++ b/solution.py
@@ -101,7 +101,12 @@
     far_out,
     far_in,
     mix,
-    mix_in,
+    mix_a,
+    mix_b,
+    fin_a,
+    fin_b,
+    sum_a,
+    sum_b,
     back,
     back_in,
     probs,
@@ -122,12 +127,18 @@
     near_r,
     far_s,
     far_r,
-    mix_s,
-    mix_r,
+    a1_s,
+    a1_r,
+    b1_s,
+    b1_r,
+    a2_s,
+    a2_r,
+    b2_s,
+    b2_r,
     back_s,
     back_r,
 ):
-    sects, groups, spans, near, far, cap = sizes
+    sects, groups, spans, near, far, cap, split = sizes
     rows = grad_out.shape[0]
     hidden = w_up.shape[0]
     cols = queries.shape[0]
@@ -135,14 +146,8 @@
     x, g, y = lax.axis_index("sect"), lax.axis_index("grp"), lax.axis_index("span")
     g_hi, g_lo = g // near, g % near
 
-    def at_xy(dx, dy):
-        return ((x + dx) % sects, g, (y + dy) % spans)
-
-    def hops(pair):
-        return min(pair[0], sects - pair[0]) + min(pair[1], spans - pair[1])
-
-    others = [(dx, dy) for dx in range(sects) for dy in range(spans) if dx or dy]
-    others.sort(key=hops, reverse=True)
+    def at_x(d):
+        return ((x + d) % sects, g, y)
 
     def at_y(d):
         return (x, g, (y + d) % spans)
@@ -193,9 +198,10 @@
     barrier = pltpu.get_barrier_semaphore()
     far_steps = sorted({1 % far, far - 1})
     peers = [at_far(d) for d in far_steps]
+    peers += [at_y(d) for d in range(1, spans)]
     peers += [at_near(d) for d in range(1, near)]
     peers += [at_g(1), at_g(-1)]
-    peers += [at_xy(dx, dy) for dx, dy in others]
+    peers += [at_x(d) for d in range(1, sects)]
     def signal(sem, peer):
         pl.semaphore_signal(sem, inc=1, device_id=peer, device_id_type=pl.DeviceIdType.MESH)
 
@@ -344,19 +350,68 @@
     unpacker = jnp.where(place == (iota((slots, rows), 1) + 1).astype(F32), 1.0, 0.0)
     grad_hidden = dot(unpacker.astype(BF16), arrived[:, :hidden], FIRST)
     grad_pre = (grad_hidden * slopes[...]).astype(BF16)
-    mix_copies = []
-    for dx, dy in others:
+    top, low = pl.ds(0, split), pl.ds(split, rows - split)
+    a_copies, b_copies = {}, {}
+    pairs = [(dx, dy) for dx in far_first(sects) for dy in far_first(spans)]
+    pairs.sort(key=lambda d: -min(d[0], sects - d[0]) - min(d[1], spans - d[1]))
+    pairs += [(dx, 0) for dx in far_first(sects)] + [(0, dy) for dy in far_first(spans)]
+    for dx, dy in pairs + [(0, 0)]:
         owner = ((x + dx) % sects) * spans + (y + dy) % spans
-        i = dx * spans + dy - 1
-        mix[i] = dot(grad_pre, wu[owner]).astype(BF16)
-        mix_copies.append(
-            (i, send(mix.at[i], mix_in.at[i], mix_s.at[i], mix_r.at[i], at_xy(dx, dy)))
-        )
-    share = dot(grad_pre, wu[x * spans + y])
-    for i, copy in mix_copies:
+        mix[dx, dy] = dot(grad_pre, wu[owner]).astype(BF16)
+        if dx:
+            a_copies[dx, dy] = send(
+                mix.at[dx, dy, top, :],
+                mix_a.at[dx - 1, dy],
+                a1_s.at[dx - 1, dy],
+                a1_r.at[dx - 1, dy],
+                at_x(dx),
+            )
+        if dy:
+            b_copies[dx, dy] = send(
+                mix.at[dx, dy, low, :],
+                mix_b.at[dy - 1, dx],
+                b1_s.at[dy - 1, dx],
+                b1_r.at[dy - 1, dx],
+                at_y(dy),
+            )
+    a2_copies, b2_copies = [], []
+
+    def sum_top(dy):
+        total = mix[0, dy, top, :].astype(F32)
+        for dx in far_first(sects):
+            a_copies[dx, dy].wait_recv()
+            total = total + mix_a[dx - 1, dy].astype(F32)
+        return total
+
+    def sum_low(dx):
+        total = mix[dx, 0, low, :].astype(F32)
+        for dy in far_first(spans):
+            b_copies[dx, dy].wait_recv()
+            total = total + mix_b[dy - 1, dx].astype(F32)
+        return total
+
+    for i in range(max(sects, spans) - 1):
+        if i < sects - 1:
+            d = far_first(sects)[i]
+            sum_b[d - 1] = sum_low(d).astype(BF16)
+            b2_copies.append(
+                send(sum_b.at[d - 1], fin_b.at[d - 1], b2_s.at[d - 1], b2_r.at[d - 1], at_x(d))
+            )
+        if i < spans - 1:
+            d = far_first(spans)[i]
+            sum_a[d - 1] = sum_top(d).astype(BF16)
+            a2_copies.append(
+                send(sum_a.at[d - 1], fin_a.at[d - 1], a2_s.at[d - 1], a2_r.at[d - 1], at_y(d))
+            )
+    share_b, share_a = sum_low(0), sum_top(0)
+    for copy in a2_copies + b2_copies:
         copy.wait_recv()
-        share = share + mix_in[i].astype(F32)
-    share = share.astype(BF16)
+    for d in range(spans - 1):
+        share_a = share_a + fin_a[d].astype(F32)
+    for d in range(sects - 1):
+        share_b = share_b + fin_b[d].astype(F32)
+    share = jnp.concatenate([share_a, share_b], 0).astype(BF16)
+
     grad_attn = jnp.zeros((cols, patches), F32)
     for p in range(4):
         grad_attn = grad_attn + dot(share[:, p * cols : (p + 1) * cols], spread[p], FIRST)
@@ -426,13 +481,14 @@
     far = groups // near
     cap = rows // min(groups, rows // 2)
     slots = groups * cap
+    split = (rows * 5 // 8 // 16) * 16 if rows >= 32 else rows // 2
     width = 4 * cols
     wide = hidden + LABEL_LANES
     dma = pltpu.SemaphoreType.DMA
     vmem = pltpu.VMEM
     some = pl.BlockSpec(memory_space=pl.ANY)
     out = jax.ShapeDtypeStruct((cols, patches), BF16)
-    sizes = (sects, groups, spans, near, far, cap)
+    sizes = (sects, groups, spans, near, far, cap, split)
     outs = pl.pallas_call(
         functools.partial(kernel, sizes),
         out_shape=(out, out, out),
@@ -455,8 +511,13 @@
             vmem((slots, wide), BF16),
             vmem((slots, wide), BF16),
             vmem((slots, wide), BF16),
-            vmem((sects * spans - 1, rows, width), BF16),
-            vmem((sects * spans - 1, rows, width), BF16),
+            vmem((sects, spans, rows, width), BF16),
+            vmem((sects - 1, spans, split, width), BF16),
+            vmem((spans - 1, sects, rows - split, width), BF16),
+            vmem((spans - 1, split, width), BF16),
+            vmem((sects - 1, rows - split, width), BF16),
+            vmem((spans - 1, split, width), BF16),
+            vmem((sects - 1, rows - split, width), BF16),
             vmem((2, 2, cols, patches), BF16),
             vmem((2, 2, cols, patches), BF16),
             vmem((3, patches, patches), F32),
@@ -477,8 +538,14 @@
             dma((near - 1,)),
             dma((far - 1,)),
             dma((far - 1,)),
-            dma((sects * spans - 1,)),
-            dma((sects * spans - 1,)),
+            dma((sects - 1, spans)),
+            dma((sects - 1, spans)),
+            dma((spans - 1, sects)),
+            dma((spans - 1, sects)),
+            dma((spans - 1,)),
+            dma((spans - 1,)),
+            dma((sects - 1,)),
+            dma((sects - 1,)),
             dma((2, 2)),
             dma((2, 2)),
         ],

time: 67.2 us -> 65.2 us (0.970)
  Pallas kernels: 66.4 us -> 64.4 us
    pallas_call x1, Pallas kernels: 64.8 us -> 62.8 us  [on_device(): pl.pallas_call(functools.partial(kernel, sizes), out_shape=(out, out, out...]
where the time goes in v6:
time: 65.2 us; the launch traced here: 65 us
  Pallas kernels  64.4 us (99%)
    pallas_call x1, Pallas kernels, on_device(): pl.pallas_call(functools.partial(kernel, sizes), out_shape=(out, out, out...  62.8 us
    pallas_call x1, Pallas kernels, on_device(): pl.pallas_call(move, out_shape=(out, out, out), in_specs=[pl.BlockSpec(me...  1.56 us

profile of v6, /device:TPU:1, one launch (start us, length us, event | category | flops | bytes accessed | tf_op | source)
XLA Modules:
  0.0 65.0 jit_solution(5381432195167045210)
XLA Ops:
  0.6 62.8 %merger_attention_backward.1 = (bf16[80,320]{1,0:T(8,128)(2,1)}, bf16[80,320]{1,0:T(8,128)(2,1)}, bf16[80,320]{1,0:T(8,128)(2,1)}) custom-call(bf16[80,2048]{1,0:T(8,128)(2,1)} %grad_out.1, s32[1,80]{1,0:T(1,128)} %bitcast.14, bf16[1280,2048]{1,0:T(8,128)(2,1)} %w_down.1, bf16[80,320]{1,0:T(8,128)(2,1)} %pre_act.1, bf16[320,5120]{1,0:T(8,128)(2,1)} %bitcast.9, ...), custom_call_target="tpu_custom_call" | custom-call | tf_op jit(solution)/shard_map/merger_attention_backward/pallas_call | solution.py:492
  63.5 1.6 %gradients_out.1 = (bf16[80,320]{1,0:T(8,128)(2,1)}, bf16[80,320]{1,0:T(8,128)(2,1)}, bf16[80,320]{1,0:T(8,128)(2,1)}) custom-call(bf16[80,320]{1,0:T(8,128)(2,1)} %get-tuple-element.9.refs_0_, bf16[80,320]{1,0:T(8,128)(2,1)} %get-tuple-element.10.refs_1_, bf16[80,320]{1,0:T(8,128)(2,1)} %get-tuple-element.11.refs_2_), custom_call_target="tpu_custom_call" | custom-call | tf_op jit(solution)/shard_map/gradients_out/pallas_call | solution.py:567

commit v7 on v6

--- a/solution.py
+++ b/solution.py
@@ -193,7 +193,6 @@
     load_len = load(lengths, lens, load_sem.at[2])
     load_q = load(queries, qs, load_sem.at[3])
     load_pre = load(pre_act, pre, load_sem.at[6])
-    load_wt = load(w_up, wt, load_sem.at[7])
 
     barrier = pltpu.get_barrier_semaphore()
     far_steps = sorted({1 % far, far - 1})
@@ -225,6 +224,7 @@
         part_copies.append(
             send(part.at[d - 1], part_in.at[d - 1], part_s.at[d - 1], part_r.at[d - 1], at_y(d))
         )
+    load_wt = load(w_up, wt, load_sem.at[7])
     load_k.wait()
     load_v.wait()
     halo_copies = []

time: 65.2 us -> 65.2 us (level)
  no operation moved by 1% of the time
where the time goes in v7:
time: 65.2 us; the launch traced here: 65 us
  Pallas kernels  64.4 us (99%)
    pallas_call x1, Pallas kernels, on_device(): pl.pallas_call(functools.partial(kernel, sizes), out_shape=(out, out, out...  62.8 us
    pallas_call x1, Pallas kernels, on_device(): pl.pallas_call(move, out_shape=(out, out, out), in_specs=[pl.BlockSpec(me...  1.56 us

profile of v7, /device:TPU:1, one launch (start us, length us, event | category | flops | bytes accessed | tf_op | source)
XLA Modules:
  0.0 65.0 jit_solution(4094470203485462612)
XLA Ops:
  0.6 62.8 %merger_attention_backward.1 = (bf16[80,320]{1,0:T(8,128)(2,1)}, bf16[80,320]{1,0:T(8,128)(2,1)}, bf16[80,320]{1,0:T(8,128)(2,1)}) custom-call(bf16[80,2048]{1,0:T(8,128)(2,1)} %grad_out.1, s32[1,80]{1,0:T(1,128)} %bitcast.14, bf16[1280,2048]{1,0:T(8,128)(2,1)} %w_down.1, bf16[80,320]{1,0:T(8,128)(2,1)} %pre_act.1, bf16[320,5120]{1,0:T(8,128)(2,1)} %bitcast.9, ...), custom_call_target="tpu_custom_call" | custom-call | tf_op jit(solution)/shard_map/merger_attention_backward/pallas_call | solution.py:492
  63.5 1.6 %gradients_out.1 = (bf16[80,320]{1,0:T(8,128)(2,1)}, bf16[80,320]{1,0:T(8,128)(2,1)}, bf16[80,320]{1,0:T(8,128)(2,1)}) custom-call(bf16[80,320]{1,0:T(8,128)(2,1)} %get-tuple-element.9.refs_0_, bf16[80,320]{1,0:T(8,128)(2,1)} %get-tuple-element.10.refs_1_, bf16[80,320]{1,0:T(8,128)(2,1)} %get-tuple-element.11.refs_2_), custom_call_target="tpu_custom_call" | custom-call | tf_op jit(solution)/shard_map/gradients_out/pallas_call | solution.py:567

commit v8 on v7

--- a/solution.py
+++ b/solution.py
@@ -185,14 +185,13 @@
     load_go = load(grad_out, go, load_sem.at[0])
     load_dst = load(dest, dst, load_sem.at[1])
     load_wd = []
-    load_k = load(keys, kx.at[1], load_sem.at[4])
-    load_v = load(values, vx.at[1], load_sem.at[5])
-    for d in order_y:
+
+    def load_chunk(d):
         chunk = pl.ds(pl.multiple_of(((y + d) % spans) * hidden, 16), hidden)
         load_wd.append(load(w_down.at[chunk, :], wd.at[chunk, :], down_sem.at[d]))
-    load_len = load(lengths, lens, load_sem.at[2])
-    load_q = load(queries, qs, load_sem.at[3])
-    load_pre = load(pre_act, pre, load_sem.at[6])
+
+    for d in order_y[:2]:
+        load_chunk(d)
 
     barrier = pltpu.get_barrier_semaphore()
     far_steps = sorted({1 % far, far - 1})
@@ -209,8 +208,16 @@
 
     load_go.wait()
     part_copies = []
-    for d, loaded in zip(order_y, load_wd):
-        loaded.wait()
+    for i, d in enumerate(order_y):
+        load_wd[i].wait()
+        if i + 2 < len(order_y):
+            load_chunk(order_y[i + 2])
+        elif i + 2 == len(order_y):
+            load_k = load(keys, kx.at[1], load_sem.at[4])
+            load_v = load(values, vx.at[1], load_sem.at[5])
+            load_len = load(lengths, lens, load_sem.at[2])
+            load_q = load(queries, qs, load_sem.at[3])
+            load_pre = load(pre_act, pre, load_sem.at[6])
         chunk = pl.ds(pl.multiple_of(((y + d) % spans) * hidden, 16), hidden)
         product = dot(go[...], wd[chunk, :], LAST)
         if d == 0:
@@ -219,8 +226,8 @@
         part[d - 1] = product.astype(BF16)
         if not part_copies:
             pl.semaphore_wait(barrier, len(peers))
-            for i, step in enumerate(far_steps):
-                signal(ready.at[0, i], at_far(step))
+            for j, step in enumerate(far_steps):
+                signal(ready.at[0, j], at_far(step))
         part_copies.append(
             send(part.at[d - 1], part_in.at[d - 1], part_s.at[d - 1], part_r.at[d - 1], at_y(d))
         )

time: 65.2 us -> 65.3 us (level)
  no operation moved by 1% of the time
where the time goes in v8:
time: 65.3 us; the launch traced here: 65 us
  Pallas kernels  64.4 us (99%)
    pallas_call x1, Pallas kernels, on_device(): pl.pallas_call(functools.partial(kernel, sizes), out_shape=(out, out, out...  62.8 us
    pallas_call x1, Pallas kernels, on_device(): pl.pallas_call(move, out_shape=(out, out, out), in_specs=[pl.BlockSpec(me...  1.56 us

profile of v8, /device:TPU:1, one launch (start us, length us, event | category | flops | bytes accessed | tf_op | source)
XLA Modules:
  0.0 65.0 jit_solution(15270860211039581487)
XLA Ops:
  0.6 62.8 %merger_attention_backward.1 = (bf16[80,320]{1,0:T(8,128)(2,1)}, bf16[80,320]{1,0:T(8,128)(2,1)}, bf16[80,320]{1,0:T(8,128)(2,1)}) custom-call(bf16[80,2048]{1,0:T(8,128)(2,1)} %grad_out.1, s32[1,80]{1,0:T(1,128)} %bitcast.14, bf16[1280,2048]{1,0:T(8,128)(2,1)} %w_down.1, bf16[80,320]{1,0:T(8,128)(2,1)} %pre_act.1, bf16[320,5120]{1,0:T(8,128)(2,1)} %bitcast.9, ...), custom_call_target="tpu_custom_call" | custom-call | tf_op jit(solution)/shard_map/merger_attention_backward/pallas_call | solution.py:499
  63.4 1.6 %gradients_out.1 = (bf16[80,320]{1,0:T(8,128)(2,1)}, bf16[80,320]{1,0:T(8,128)(2,1)}, bf16[80,320]{1,0:T(8,128)(2,1)}) custom-call(bf16[80,320]{1,0:T(8,128)(2,1)} %get-tuple-element.9.refs_0_, bf16[80,320]{1,0:T(8,128)(2,1)} %get-tuple-element.10.refs_1_, bf16[80,320]{1,0:T(8,128)(2,1)} %get-tuple-element.11.refs_2_), custom_call_target="tpu_custom_call" | custom-call | tf_op jit(solution)/shard_map/gradients_out/pallas_call | solution.py:574
